TPU v7x, 128 devices: a whole 4x4x4 slice. The times are simulated.
128 devices in a mesh: lat: 16 (over x, z), lon: 8 (over y, core).
Axes of the slice: x: 4, y: 4, z: 4, core: 2. Of those that a mesh axis runs over, the one named last changes fastest.
Arguments:
- grid_fields: float32 [8, 32, 6144], P(None, 'lat', 'lon'), may hold values from -6 to 6
- sun_cosine: float32 [32, 6144], P('lat', 'lon'), may hold values from 0.1 to 1
- surface_albedo: float32 [32, 6144], P('lat', 'lon'), may hold values from 0.05 to 0.8
- gas_absorb: float32 [112], replicated, may hold values from 0.02 to 4
- solar_weight: float32 [112], replicated, may hold values from 0.1 to 1
- helper_map: int32 [32, 48], P('lat', 'lon'), may hold values from -1 to 127, as said below
- row_lat: int32 [32], replicated, may hold values from 1008 to 1551, as said below
- wave_owner: int32 [1280], replicated, may hold values from 0 to 15, as said below
Outputs:
- spectral: float32 [1920, 8, 2, 1280], P(('lat', 'lon'))
Inputs may be any that keep to these rules, and one draw needn't show every extreme that they name: `helper_map`: the lit blocks are the same 48 / 2 cyclically consecutive block columns in every row. Lit blocks are numbered in the order of devices along lat+lon and within a device by row, then block, and the k-th goes to helper k mod 128: a device sends at most 1 lit blocks to one helper (a device whose blocks are all lit does so), and every helper receives exactly 6 lit blocks. `row_lat`: increasing and distinct, 32 of the 544 latitudes nearest the equator, always holding the first and last of them and latitude 2560 / 2 - 1. `wave_owner`: half of the owners hold exactly 120 wavenumbers and the other half exactly 40; which wavenumbers is arbitrary.
All inputs are finite; a program needn't handle non-finite values.
Results may differ from a plain program's by a relative error of at most 0.0006.
Values sent between devices are 32-bit elements; how exact they have to be, the bound alone decides.
No kernel may reach another device: no remote copies, remote signals or barrier semaphores. Data moves between devices by JAX's collectives and lax.ppermute only.
A program may use at most 64 MiB of HBM per device.

v0:
```python
import math

import jax
import jax.numpy as jnp
from jax import lax
from jax.sharding import PartitionSpec as P

LEV = 4
BLOCK = 128
NLAT_FULL = 2560
MW = 1280


diffusivity = 1.66
scatter_share = 0.2
heat_gain = 10.0
highest = lax.Precision.HIGHEST


def radiate(humidity, sun_cos, ground, gas_absorb, solar_weight):
    shares = solar_weight / jnp.sum(solar_weight)
    levels = humidity.shape[0]
    directs = [shares[:, None] * sun_cos[None, :]]
    down_flux = [jnp.zeros_like(directs[0])]
    trans_list = []
    sources = []
    for layer_idx in range(levels):
        optical = gas_absorb[:, None] * jax.nn.softplus(humidity[layer_idx])[None, :]
        trans_dir = jnp.exp(-optical / sun_cos[None, :])
        trans_dif = jnp.exp(-diffusivity * optical)
        source = scatter_share * directs[-1] * (1.0 - trans_dir)
        down_flux.append(down_flux[-1] * trans_dif + source)
        directs.append(directs[-1] * trans_dir)
        trans_list.append(trans_dif)
        sources.append(source)
    upward = [None] * (levels + 1)
    upward[levels] = ground[None, :] * (directs[levels] + down_flux[levels])
    for layer_idx in range(levels - 1, -1, -1):
        upward[layer_idx] = upward[layer_idx + 1] * trans_list[layer_idx] + sources[layer_idx]
    net_flux = [
        directs[level_idx] + down_flux[level_idx] - upward[level_idx]
        for level_idx in range(levels + 1)
    ]
    heating = [
        heat_gain * jnp.sum(net_flux[level_idx] - net_flux[level_idx + 1], axis=0)
        for level_idx in range(levels)
    ]
    return jnp.stack(heating)


def radiate_blocks(inputs, gas_absorb, solar_weight):
    block_count = inputs.shape[0]
    group_size = math.gcd(block_count, 16)

    def radiate_one_group(piece_data):
        flattened = piece_data.transpose(1, 0, 2).reshape(LEV + 2, group_size * BLOCK)
        heated = radiate(
            flattened[:LEV], flattened[LEV], flattened[LEV + 1], gas_absorb, solar_weight
        )
        return heated.reshape(LEV, group_size, BLOCK).transpose(1, 0, 2)

    pieces = inputs.reshape(block_count // group_size, group_size, LEV + 2, BLOCK)
    return lax.map(radiate_one_group, pieces).reshape(block_count, LEV, BLOCK)


def inner_table(count):
    wave_ids = jnp.arange(MW, dtype=jnp.int32)
    offsets = jnp.arange(BLOCK, dtype=jnp.int32)
    phase_int = offsets[:, None] * wave_ids[None, :] % count
    angles = phase_int.astype(jnp.float32) * (2.0 * math.pi) / count.astype(jnp.float32)
    return jnp.concatenate([jnp.cos(angles), -jnp.sin(angles)], axis=1)


def block_twiddle(count, block_ids):
    wave_ids = jnp.arange(MW, dtype=jnp.int32)
    phase_int = block_ids[:, None] * BLOCK * wave_ids[None, :] % count
    angles = phase_int.astype(jnp.float32) * (2.0 * math.pi) / count.astype(jnp.float32)
    return (jnp.cos(angles), jnp.sin(angles))


def row_transform(rows_x, counts, first_block):
    row_count, vector_count, col_count = rows_x.shape
    block_count = col_count // BLOCK
    group_size = math.gcd(row_count, 2)
    block_ids = first_block + jnp.arange(block_count, dtype=jnp.int32)
    col_ids = first_block * BLOCK + jnp.arange(col_count, dtype=jnp.int32)

    def row_one_group(pair_args):
        values, lengths = pair_args
        masked = jnp.where(col_ids[None, None, :] < lengths[:, None, None], values, 0.0)
        pieces = masked.reshape(group_size, vector_count, block_count, BLOCK)
        tables = jax.vmap(inner_table)(lengths)
        partial_y = jnp.einsum("gvab,gbm->gvam", pieces, tables, precision=highest)
        cos_t, sin_t = jax.vmap(lambda length: block_twiddle(length, block_ids))(lengths)
        real_y = partial_y[..., :MW]
        imag_y = partial_y[..., MW:]
        cos_b = cos_t[:, None]
        sin_b = sin_t[:, None]
        real_x = jnp.sum(cos_b * real_y + sin_b * imag_y, axis=2)
        imag_x = jnp.sum(cos_b * imag_y - sin_b * real_y, axis=2)
        return jnp.stack([real_x, imag_x], axis=2)

    transformed = lax.map(
        row_one_group,
        (
            rows_x.reshape(row_count // group_size, group_size, vector_count, col_count),
            counts.reshape(row_count // group_size, group_size),
        ),
    )
    return transformed.reshape(row_count, vector_count, 2, MW)


def legendre(inputs, wave_ids, cos_lat, sin_lat):
    slot_count, col_count, row_count = inputs.shape
    mfloat = wave_ids.astype(jnp.float32)
    log_start = 0.5 * (
        lax.lgamma(mfloat + 1.5)
        - lax.lgamma(jnp.ones_like(mfloat) * 1.5)
        - lax.lgamma(mfloat + 1.0)
        + jnp.log(2.0 - (wave_ids == 0).astype(jnp.float32))
    )
    start_vals = jnp.exp(log_start[:, None] + mfloat[:, None] * jnp.log(sin_lat)[None, :])
    unroll = math.gcd(MW, 64)
    turn_count = MW // unroll

    def advance(previous, current, step_idx):
        degree = mfloat + (step_idx + 1).astype(jnp.float32)
        square = degree * degree - mfloat * mfloat
        factor_a = jnp.sqrt((4.0 * degree * degree - 1.0) / square)
        factor_b = jnp.sqrt(
            (2.0 * degree + 1.0)
            * (degree - 1.0 - mfloat)
            * (degree - 1.0 + mfloat)
            / ((2.0 * degree - 3.0) * square)
        )
        return factor_a[:, None] * cos_lat[None, :] * current - factor_b[:, None] * previous

    def one_turn(carried, turn_idx):
        previous, current = carried
        rows_out = []
        for offset in range(unroll):
            rows_out.append(current)
            previous, current = (current, advance(previous, current, turn_idx * unroll + offset))
        stacked = jnp.stack(rows_out, axis=1)
        contrib = jnp.einsum("skr,scr->sck", stacked, inputs, precision=highest)
        return ((previous, current), contrib)

    final_state, blocks = lax.scan(
        one_turn, (jnp.zeros_like(start_vals), start_vals), jnp.arange(turn_count, dtype=jnp.int32)
    )
    return blocks.transpose(1, 2, 0, 3).reshape(slot_count, col_count, MW)


def slot_table(wave_owner, owners, slot_cap):
    wave_ids = jnp.arange(MW, dtype=jnp.int32)
    same_owner = (wave_owner[None, :] == wave_owner[:, None]) & (
        wave_ids[None, :] < wave_ids[:, None]
    )
    wave_rank = jnp.sum(same_owner.astype(jnp.int32), axis=1)
    keyed = wave_owner * slot_cap + wave_rank
    slots = jnp.arange(owners * slot_cap, dtype=jnp.int32)
    slot_hits = keyed[None, :] == slots[:, None]
    wave_of = jnp.sum(jnp.where(slot_hits, wave_ids[None, :], 0), axis=1)
    slot_used = jnp.any(slot_hits, axis=1)
    return (wave_of, slot_used)


def shards(
    grid_fields,
    sun_cosine,
    surface_albedo,
    gas_absorb,
    solar_weight,
    helper_map,
    row_lat,
    wave_owner,
):
    lat_size = lax.axis_size("lat")
    lon_size = lax.axis_size("lon")
    helpers = lat_size * lon_size
    lat_me = lax.axis_index("lat")
    lon_me = lax.axis_index("lon")
    field_count, rows_dev, seg_len = grid_fields.shape
    seg_blocks = seg_len // BLOCK
    blocks_dev = rows_dev * seg_blocks
    rows_total = rows_dev * lat_size
    vector_group = field_count // lon_size
    humidity = grid_fields[:LEV].reshape(LEV, blocks_dev, BLOCK).transpose(1, 0, 2)
    block_sun = sun_cosine.reshape(blocks_dev, 1, BLOCK)
    block_ground = surface_albedo.reshape(blocks_dev, 1, BLOCK)
    block_data = jnp.concatenate([humidity, block_sun, block_ground], axis=1)
    targets = helper_map.reshape(blocks_dev)
    lit_block = targets >= 0
    tendency = jnp.where(
        lit_block[:, None, None], radiate_blocks(block_data, gas_absorb, solar_weight), 0.0
    )
    tendency_grid = tendency.transpose(1, 0, 2).reshape(LEV, rows_dev, seg_len)
    heated_fields = jnp.concatenate([grid_fields[:LEV], grid_fields[LEV:] + tendency_grid], axis=0)
    counts_all = 20 + 4 * jnp.minimum(row_lat, NLAT_FULL - 1 - row_lat)
    my_counts = lax.dynamic_slice_in_dim(counts_all, lat_me * rows_dev, rows_dev)
    colatitude = math.pi * (row_lat.astype(jnp.float32) + 0.5) / NLAT_FULL
    cos_lat = jnp.cos(colatitude)
    sin_lat = jnp.sin(colatitude)
    full_rows = lax.all_to_all(heated_fields, "lon", split_axis=0, concat_axis=2, tiled=True)
    spectra = row_transform(full_rows.transpose(1, 0, 2), my_counts, 0)
    row_scale = 1.0 / jnp.sqrt((rows_total * my_counts).astype(jnp.float32))
    spectra = spectra * row_scale[:, None, None, None]
    slot_cap = 3 * MW // (2 * lat_size)
    per_dev = slot_cap // lon_size
    wave_of, slot_used = slot_table(wave_owner, lat_size, slot_cap)
    picked = jnp.where(slot_used, spectra[..., wave_of], 0.0)
    outgoing_waves = picked.reshape(
        rows_dev, vector_group * 2, lat_size, lon_size, per_dev
    ).transpose(2, 3, 4, 1, 0)
    incoming_waves = lax.all_to_all(
        outgoing_waves.reshape(helpers, per_dev * vector_group * 2 * rows_dev),
        ("lat", "lon"),
        split_axis=0,
        concat_axis=0,
        tiled=True,
    )
    arranged = (
        incoming_waves.reshape(lat_size, lon_size, per_dev, vector_group, 2, rows_dev)
        .transpose(2, 1, 3, 4, 0, 5)
        .reshape(per_dev, field_count * 2, rows_total)
    )
    first_slot = lat_me * slot_cap + lon_me * per_dev
    my_waves = lax.dynamic_slice_in_dim(wave_of, first_slot, per_dev)
    my_used = lax.dynamic_slice_in_dim(slot_used, first_slot, per_dev)
    coeffs = legendre(arranged, my_waves, cos_lat, sin_lat)
    degree_ok = my_waves[:, None] + jnp.arange(MW, dtype=jnp.int32)[None, :] <= MW - 1
    result = jnp.where(degree_ok[:, None, :] & my_used[:, None, None], coeffs, 0.0)
    return result.reshape(per_dev, field_count, 2, MW)


def solution(mesh):
    placed = (
        P(None, "lat", "lon"),
        P("lat", "lon"),
        P("lat", "lon"),
        P(),
        P(),
        P("lat", "lon"),
        P(),
        P(),
    )
    return jax.shard_map(
        shards,
        mesh=mesh,
        in_specs=placed,
        out_specs=P(("lat", "lon"), None, None, None),
        check_vma=False,
    )
```

profile of v0, /device:TPU:1, one launch (start us, length us, event | category | flops | bytes accessed | tf_op | source)
XLA Modules:
  0.0 1499.4 jit_solution(18212157780955816927)
XLA Ops:
  3.6 8.7 while.33
  13.2 6.0 all-to-all-start
  26.3 17.9 %fusion.326 = (f32[2,128,1280]{2,1,0:T(8,128)S(1)}, f32[2,128,1280]{2,1,0:T(8,128)S(1)}) fusion(f32[2]{0:T(128)S(1)} %get-tuple-element.1294, pred[2]{0:T(512)(128)(4,1)} %broadcast_compare_fusion.1, s32[2]{0:T(128)S(1)} %get-tuple-element.1293, s32[128,1280]{1,0:T(8,128)S(1)} %iota_multiply_fusion), kind=kLoop, calls=%fused_computation.632 | loop fusion | flops 3604480 | bytes 3276818 | tf_op jit(solution)/shard_map/while/body/eval_jaxpr/vmap()/cos | solution.py:71
  47.2 2.2 convolution_bitcast_fusion.1
  49.5 7.0 add_reduce_fusion
  57.2 6.7 gather_fusion
  63.9 3.2 copy.2485
  68.8 10.3 all-to-all-start.1
  79.2 9.3 all-to-all-done.1
  90.4 1400.8 %while.34 = (s32[]{:T(128)}, f32[15,32]{1,0:T(8,128)S(1)}, f32[15,32]{1,0:T(8,128)S(1)}, f32[20,15,16,64]{3,2,1,0:T(8,128)}, s32[20]{0:T(128)S(1)}, /*index=5*/f...) while((s32[]{:T(128)}, f32[15,32]{1,0:T(8,128)S(1)}, ...), condition=%wide.region_13.14_spmd.clone, body=%wide.region_12.13_spmd.clone.sunk | while | flops 6080772 | bytes 1095664 | solution.py:148
  148.4 10.1 stack.543
  158.5 1.9 fusion.392
  168.0 1.6 copy.2562
  218.5 10.1 stack.543
  228.6 1.9 fusion.392
  288.5 10.1 stack.543
  298.6 1.9 fusion.392
  308.1 1.6 copy.2562
  358.5 10.1 stack.543
  368.6 1.9 fusion.392
  428.6 10.1 stack.543
  438.7 1.9 fusion.392
  448.2 1.6 copy.2562
  498.6 10.1 stack.543
  508.7 1.9 fusion.392
  518.2 1.6 copy.2562
  568.7 10.1 stack.543
  578.8 1.9 fusion.392
  588.3 1.6 copy.2562
  638.7 10.1 stack.543
  648.8 1.9 fusion.392
  658.3 1.6 copy.2562
  708.8 10.1 stack.543
  718.9 1.9 fusion.392
  728.4 1.6 copy.2562
  778.8 10.1 stack.543
  788.9 1.9 fusion.392
  848.9 10.1 stack.543
  858.9 1.9 fusion.392
  918.9 10.1 stack.543
  929.0 1.9 fusion.392
  988.9 10.1 stack.543
  999.0 1.9 fusion.392
  1008.6 1.6 copy.2562
  1059.0 10.1 stack.543
  1069.1 1.9 fusion.392
  1078.6 1.6 copy.2562
  1129.1 10.1 stack.543
  1139.1 1.9 fusion.392
  1148.7 1.6 copy.2562
  1199.1 10.1 stack.543
  1209.2 1.9 fusion.392
  1218.7 1.6 copy.2562
  1269.1 10.1 stack.543
  1279.2 1.9 fusion.392
  1339.2 10.1 stack.543
  1349.3 1.9 fusion.392
  1409.2 10.1 stack.543
  1419.3 1.9 fusion.392
  1479.2 10.1 stack.543
  1489.3 1.9 fusion.392
  1491.2 2.5 copy.2484
  1493.7 2.3 reshape.2914
  1496.0 2.9 broadcast_select_fusion
  (2423 shorter events, 1149.7 us)
Async XLA Ops:
  3.6 15.6 %copy-start.31 = (s32[32]{0:T(128)S(1)}, s32[32]{0:T(128)}, u32[]{:S(2)}) copy-start(s32[32]{0:T(128)} %param.18) | copy-start | bytes 388
  3.6 17.4 %copy-start.20 = (s32[1280]{0:T(1024)S(1)}, s32[1280]{0:T(1024)}, u32[]{:S(2)}) copy-start(s32[1280]{0:T(1024)} %param.19) | copy-start | bytes 15364
  13.2 33.1 %all-to-all-start = ((f32[8,2,768]{2,1,0:T(2,128)}), f32[8,2,768]{2,1,0:T(2,128)}, u32[]{:S(2)}, u32[]{:S(2)}) async-start(f32[8,2,768]{2,1,0:T(2,128)} %pad_maximum_fusion.1), calls=%async_computation | async-start | bytes 98304 | tf_op jit(solution)/shard_map/all_to_all | solution.py:204
  19.8 24.4 %copy-start.21 = (f32[2]{0:T(128)}, f32[2]{0:T(128)S(1)}, u32[]{:S(2)}) copy-start(f32[2]{0:T(128)S(1)} %get-tuple-element.1294) | copy-start | bytes 28
  63.8 15.3 %copy-start.28 = (f32[32]{0:T(128)S(1)}, f32[32]{0:T(128)}, u32[]{:S(2)}) copy-start(f32[32]{0:T(128)} %get-tuple-element.1296) | copy-start | bytes 388
  63.9 15.3 %copy-start.29 = (f32[15]{0:T(128)S(1)}, f32[15]{0:T(128)}, u32[]{:S(2)}) copy-start(f32[15]{0:T(128)} %fusion.352) | copy-start | bytes 184
  68.8 19.8 %all-to-all-start.1 = ((f32[128,1,60]{2,1,0:T(1,128)}), f32[128,1,60]{2,1,0:T(1,128)S(1)}, u32[]{:S(2)}, u32[]{:S(2)}) async-start(f32[128,1,60]{2,1,0:T(1,128)} %copy.2480), calls=%async_computation.1 | async-start | bytes 131072 | tf_op jit(solution)/shard_map/all_to_all | solution.py:215
  148.4 12.0 copy-start.1
  148.4 12.0 copy-start.3
  148.4 12.0 copy-start.5
  148.4 12.0 copy-start.33
  288.5 12.0 copy-start.1
  288.5 12.0 copy-start.3
  288.5 12.0 copy-start.5
  288.5 12.0 copy-start.33
  358.5 12.0 copy-start.1
  358.5 12.0 copy-start.3
  358.5 12.0 copy-start.5
  358.5 12.0 copy-start.33
  428.6 12.0 copy-start.1
  428.6 12.0 copy-start.3
  428.6 12.0 copy-start.5
  428.6 12.0 copy-start.33
  498.6 12.0 copy-start.33
  568.7 12.0 copy-start.1
  568.7 12.0 copy-start.3
  568.7 12.0 copy-start.5
  568.7 12.0 copy-start.33
  638.7 12.0 copy-start.1
  638.7 12.0 copy-start.3
  638.7 12.0 copy-start.5
  638.7 12.0 copy-start.33
  708.8 12.0 copy-start.1
  708.8 12.0 copy-start.3
  708.8 12.0 copy-start.5
  708.8 12.0 copy-start.33
  778.8 12.0 copy-start.5
  778.8 12.0 copy-start.33
  848.8 12.0 copy-start.1
  848.8 12.0 copy-start.3
  848.8 12.0 copy-start.5
  848.9 12.0 copy-start.33
  918.9 12.0 copy-start.3
  918.9 12.0 copy-start.5
  918.9 12.0 copy-start.33
  988.9 12.0 copy-start.1
  988.9 12.0 copy-start.3
  988.9 12.0 copy-start.5
  988.9 12.0 copy-start.33
  1059.0 12.0 copy-start.1
  1059.0 12.0 copy-start.3
  1059.0 12.0 copy-start.5
  1059.0 12.0 copy-start.33
  1129.0 12.0 copy-start.1
  1129.0 12.0 copy-start.3
  1129.0 12.0 copy-start.5
  1129.0 12.0 copy-start.33
  1199.1 12.0 copy-start.33
  1269.1 12.0 copy-start.33
  1409.2 12.0 copy-start.33
  1479.2 12.0 copy-start.1
  1479.2 12.0 copy-start.3
  1479.2 12.0 copy-start.5
  1479.2 12.0 copy-start.33
  (352 other events, 996.1 us)
where the time goes:
time: 1520 us; the launch traced here: 1500 us
  local copies, waits for them, and re-layouts  1250 us (82%)
  other arithmetic  163 us (11%)
  matrix products  40 us (3%)
  loops' own time  21.8 us (1%)
  starting transfers between devices  16.3 us (1%)
    another operation x1300, local copies, waits for them, and re-layouts, one_turn(): stacked = jnp.stack(rows_out, axis=1)  1210 us
    another operation x140, other arithmetic, one_turn(): stacked = jnp.stack(rows_out, axis=1)  94.5 us
    dot_general x20, matrix products, one_turn(): contrib = jnp.einsum('skr,scr->sck', stacked, inputs, precision=highest)  37.7 us
  transfers between devices with their start and end apart: 2, of which 1 were waited for; matrix products, arithmetic and copies ran while one was open for 2% of the time, Pallas kernels for 0%

commit v1 on v0

v1 whole, which is shorter than its diff:
```python
import math

import jax
import jax.numpy as jnp
from jax import lax
from jax.experimental import pallas as pl
from jax.experimental.pallas import tpu as pltpu
from jax.sharding import PartitionSpec as P

LEV = 4
BLOCK = 128
NLAT_FULL = 2560
MW = 1280
G = 112
K = 8
SEG_BLOCKS = 6
ROWS_DEV = 2
N_LAT = 16
N_LON = 8
DESTS = N_LAT * N_LON
PER_DEV = 15
MCAP = PER_DEV * N_LON
ROWS_T = N_LAT * ROWS_DEV
LOG2E = math.log2(math.e)

f32 = jnp.float32
bf16 = jnp.bfloat16


def iota(shape, dim):
    return lax.broadcasted_iota(jnp.int32, shape, dim)


def dot(a, b, contract=(1, 0)):
    return lax.dot_general(
        a, b, (((contract[0],), (contract[1],)), ((), ())), preferred_element_type=f32
    )


def split(x):
    high = x.astype(bf16)
    return high, (x - high.astype(f32)).astype(bf16)


def sincos_turns(frac):
    quarter = jnp.round(frac * 4.0)
    r = (frac - quarter * 0.25) * (2.0 * math.pi)
    r2 = r * r
    sin_r = r + r * r2 * (-1.0 / 6 + r2 * (1.0 / 120 + r2 * (-1.0 / 5040 + r2 * (1.0 / 362880))))
    cos_r = 1.0 + r2 * (-0.5 + r2 * (1.0 / 24 + r2 * (-1.0 / 720 + r2 * (1.0 / 40320))))
    turns = quarter.astype(jnp.int32)
    odd = (turns & 1) == 1
    cos_v = jnp.where(odd, sin_r, cos_r)
    sin_v = jnp.where(odd, cos_r, sin_r)
    cos_v = jnp.where(((turns + 1) & 2) == 2, -cos_v, cos_v)
    sin_v = jnp.where((turns & 2) == 2, -sin_v, sin_v)
    return cos_v, sin_v


def slot_of(lane_q, lane_u):
    return (lane_q // 2) * 8 + lane_u * 2 + lane_q % 2


def find_slots(owner_ref, wave_ref):
    groups = MW // 128
    hits = [
        (owner_ref[:, b * 128 : (b + 1) * 128] == iota((N_LAT, 128), 0)).astype(f32)
        for b in range(groups)
    ]
    stacked = jnp.concatenate(hits, axis=0).astype(bf16)
    before = (iota((128, 128), 0) < iota((128, 128), 1)).astype(f32).astype(bf16)
    ahead = dot(stacked, before)
    total = dot(stacked, jnp.ones((128, 128), bf16))
    carry = jnp.zeros((N_LAT, 128), f32)
    table = jnp.zeros((2 * N_LAT, 128), f32)
    for b in range(groups):
        part = slice(b * N_LAT, (b + 1) * N_LAT)
        rank = jnp.sum(hits[b] * (ahead[part] + carry), axis=0, keepdims=True)
        carry = carry + total[part]
        ranked = (rank.astype(jnp.int32) == iota((128, 128), 0)).astype(f32).astype(bf16)
        number = iota((N_LAT, 128), 1) + (b * 128 + 1)
        high = ((number >> 4) << 4).astype(f32)
        low = (number & 15).astype(f32)
        both = jnp.concatenate([hits[b] * high, hits[b] * low], axis=0).astype(bf16)
        table = table + dot(both, ranked, (1, 1))
    table = table.astype(bf16)
    lane = iota((128, 128), 1)
    for u in range(4):
        index = slot_of(lane % 4, u)
        rank = ((lane // 4) % N_LON) * PER_DEV + index
        pick = ((iota((128, 128), 0) == rank) & (index < PER_DEV)).astype(f32).astype(bf16)
        found = dot(table, pick)
        found = found[:N_LAT] + found[N_LAT:]
        for g in range(4):
            own = iota((N_LAT, 128), 0) == g * 4 + iota((N_LAT, 128), 1) // 32
            wave_ref[u * 4 + g : u * 4 + g + 1, :] = jnp.sum(
                jnp.where(own, found, 0.0), axis=0, keepdims=True
            )


def front_kernel(
    fields_ref, sun_ref, ground_ref, gas_ref, weight_ref, lit_ref, row_ref, owner_ref,
    out_ref, wave_ref, gas_s, weight_s, left_s, spec_s,
):
    lat_me = lax.axis_index("lat")
    lon_me = lax.axis_index("lon")
    find_slots(owner_ref, wave_ref)

    def column(row):
        padded = jnp.concatenate([row, jnp.zeros((1, 128 - G), f32)], axis=1)
        return jnp.broadcast_to(padded, (128, 128)).T

    total_weight = jnp.sum(weight_ref[...], axis=1, keepdims=True)
    gas_s[...] = column(gas_ref[...])
    weight_s[...] = column(weight_ref[...] * (heat_gain / total_weight))

    counts = []
    for g in range(ROWS_DEV):
        row = row_ref[lat_me * ROWS_DEV + g]
        counts.append(20 + 4 * jnp.minimum(row, NLAT_FULL - 1 - row))

    for g in range(ROWS_DEV):

        def heat_block(a, carry, g=g):
            columns = pl.ds(pl.multiple_of(a * BLOCK, BLOCK), BLOCK)
            x = fields_ref[:, g, columns]
            depth = jnp.maximum(x, 0.0) + jnp.log1p(jnp.exp(-jnp.abs(x)))
            sun = sun_ref[g : g + 1, columns]
            slant = depth * (-LOG2E / sun)
            diffuse = depth * (-LOG2E * diffusivity)
            tile = lambda row: jnp.broadcast_to(row, (8, BLOCK))
            sun_b = tile(sun)
            ground_b = tile(ground_ref[g : g + 1, columns])
            slants = [tile(slant[level : level + 1]) for level in range(LEV)]
            diffuses = [tile(diffuse[level : level + 1]) for level in range(LEV)]
            sums = [jnp.zeros((8, BLOCK), f32) for _ in range(LEV)]
            for part in range(G // 8):
                gas = gas_s[part * 8 : (part + 1) * 8, :]
                weight = weight_s[part * 8 : (part + 1) * 8, :]
                direct, down = sun_b, None
                lost, sources, downs, passed = [], [], [], []
                for level in range(LEV):
                    t_dir = jnp.exp2(gas * slants[level])
                    t_dif = jnp.exp2(gas * diffuses[level])
                    absorbed = direct * (1.0 - t_dir)
                    source = scatter_share * absorbed
                    lost.append(absorbed)
                    sources.append(source)
                    downs.append(down)
                    passed.append(t_dif)
                    down = source if down is None else down * t_dif + source
                    direct = direct * t_dir
                upward = ground_b * (direct + down)
                for level in range(LEV - 1, -1, -1):
                    both = upward if downs[level] is None else downs[level] + upward
                    net = (1.0 - 2.0 * scatter_share) * lost[level] + (1.0 - passed[level]) * both
                    sums[level] = sums[level] + weight * net
                    upward = upward * passed[level] + sources[level]
            is_lit = lit_ref[g, a] >= 0
            heated = x
            for level in range(LEV):
                heat = jnp.where(is_lit, jnp.sum(sums[level], axis=0, keepdims=True), 0.0)
                heated = heated + jnp.where(iota((8, BLOCK), 0) == LEV + level, heat, 0.0)
            first = (lon_me * SEG_BLOCKS + a) * BLOCK
            heated = jnp.where(iota((8, BLOCK), 1) + first < counts[g], heated, 0.0)
            left_s[g, pl.ds(pl.multiple_of(a * 8, 8), 8), :] = heated
            return carry

        lax.fori_loop(0, SEG_BLOCKS, heat_block, 0)

    lefts = []
    for g in range(ROWS_DEV):
        high, low = split(left_s[g])
        top = jnp.concatenate([high, high], axis=1)
        bottom = jnp.concatenate([low, jnp.zeros_like(low)], axis=1)
        lefts.append(jnp.concatenate([top, bottom], axis=0))

    sub = iota((8, 128), 0)
    first_block = (lon_me * SEG_BLOCKS * BLOCK).astype(f32)
    steps = jnp.concatenate(
        [
            sub.astype(f32),
            (sub * 8).astype(f32),
            (sub * 8 + 64).astype(f32),
            (sub * BLOCK).astype(f32) + first_block,
        ],
        axis=0,
    )

    def transform(index, carry):
        wave = jnp.maximum(wave_ref[pl.ds(index, 1), :] - 1.0, 0.0)
        u = index // 4
        lanes = pl.ds(pl.multiple_of((index % 4) * 128, 128), 128)
        for g in range(ROWS_DEV):
            n = jnp.full((8, 128), counts[g], jnp.int32).astype(f32)
            inverse = 1.0 / n
            n_row, inverse_row = n[:1], inverse[:1]
            phase = steps * wave
            phase = phase - n_row * jnp.round(phase * inverse_row)
            cos_v, sin_v = sincos_turns(phase * inverse_row)
            cos_low, sin_low = cos_v[:8], sin_v[:8]
            highs, lows = [], []
            cos_h, cos_l, sin_h, sin_l = [], [], [], []
            for b in range(8):
                cos_p, sin_p = [], []
                for half in range(2):
                    at = 8 + b * 2 + half
                    cos_b, sin_b = cos_v[at : at + 1], sin_v[at : at + 1]
                    cos_p.append(cos_low * cos_b - sin_low * sin_b)
                    sin_p.append(sin_low * cos_b + cos_low * sin_b)
                high, low = split(jnp.concatenate(cos_p, axis=0))
                cos_h.append(high)
                cos_l.append(low)
                high, low = split(jnp.concatenate(sin_p, axis=0))
                sin_h.append(high)
                sin_l.append(low)
            right = jnp.concatenate(
                [
                    jnp.concatenate(cos_h + cos_l, axis=0),
                    jnp.concatenate(sin_h + sin_l, axis=0),
                ],
                axis=1,
            )
            both = dot(lefts[g], right)
            size = SEG_BLOCKS * 8
            both = both[:size] + both[size:]
            scale = lax.rsqrt(n_row * ROWS_T)
            cos_t, sin_t = cos_v[24:] * scale, sin_v[24:] * scale
            real = jnp.zeros((8, 128), f32)
            imag = jnp.zeros((8, 128), f32)
            for a in range(SEG_BLOCKS):
                c = both[a * 8 : a * 8 + 8, :128]
                s = both[a * 8 : a * 8 + 8, 128:]
                cos_a, sin_a = cos_t[a : a + 1], sin_t[a : a + 1]
                real = real + (cos_a * c - sin_a * s)
                imag = imag - (cos_a * s + sin_a * c)
            at = pl.multiple_of(u * 32 + g * 16, 16)
            spec_s[pl.ds(at, 16), lanes] = jnp.concatenate([real, imag], axis=0)
        return carry

    lax.fori_loop(0, 16, transform, 0)
    for g in range(4):
        out_ref[g * 128 : (g + 1) * 128, :] = spec_s[:, g * 128 : (g + 1) * 128].T


def recur_kernel(wave_ref, row_ref, high_ref, low_ref, poly_s):
    lat_me = lax.axis_index("lat")
    lon_me = lax.axis_index("lon")
    me = lat_me * N_LON + lon_me
    group = me // 32
    lane = iota((1, 128), 1)
    rows = jnp.zeros((1, 128), jnp.int32)
    for part in range(ROWS_DEV):
        for lat in range(N_LAT):
            rows = jnp.where(lane % 32 == part * 16 + lat, row_ref[lat * 2 + part], rows)
    angle = (NLAT_FULL / 2 - 0.5) - rows.astype(f32)
    _, x = sincos_turns(jnp.broadcast_to(angle * (1.0 / (2 * NLAT_FULL)), (4, 128)))
    log_sin = 0.5 * jnp.log1p(-x * x)

    found = []
    for q in range(4):
        total = jnp.zeros((1, 128), f32)
        for u in range(4):
            mine = wave_ref[pl.ds(u * 4 + group, 1), :]
            value = jnp.sum(
                jnp.where(lane == (me % 32) * 4 + q, mine, 0.0), axis=1, keepdims=True
            )
            total = jnp.where(lane // 32 == u, value, total)
        found.append(total)
    number = jnp.concatenate(found, axis=0)
    m = jnp.maximum(number - 1.0, 0.0)
    limit = jnp.where(number > 0.5, MW - m, 0.0)

    z = m + 1.0
    ratio = (z * (z + 1.0) * (z + 2.0) * (z + 3.0)) / (
        (z + 0.5) * (z + 1.5) * (z + 2.5) * (z + 3.5)
    )
    far = 1.0 / (z + 4.0)
    far2 = far * far
    log_ratio = (
        0.5 * jnp.log(z + 4.0)
        + far * (-1.0 / 8 + far2 * (1.0 / 192 - far2 * (1.0 / 640)))
        + jnp.log(ratio)
    )
    log_start = 0.5 * (
        log_ratio - math.lgamma(1.5) + jnp.where(m > 0.5, math.log(2.0), 0.0)
    )
    start = jnp.exp(log_start + m * log_sin)
    twice = 2.0 * m

    unroll = 16

    def turn(t, state):
        previous, current, shrink = state
        base = (t * unroll).astype(f32)
        for j in range(unroll):
            poly_s[pl.ds(pl.multiple_of(t * (unroll * 4), unroll * 4) + j * 4, 4), :] = current
            step = base + (j + 1.0)
            reach = twice + step
            degree2 = reach + step
            square = degree2 * degree2 - 1.0
            gap = step * reach
            root = lax.rsqrt(square * gap)
            grow = square * root
            previous, current = (
                current,
                (grow * x) * current - (grow * shrink) * previous,
            )
            shrink = gap * root
        return previous, current, shrink

    zero = jnp.zeros((4, 128), f32)
    lax.fori_loop(0, MW // unroll, turn, (zero, start, zero))

    for q in range(4):
        for b in range(MW // 128):
            piece = poly_s[pl.ds(b * 512 + q, 128, stride=4), :]
            within = (iota((128, 128), 0) + b * 128).astype(f32) < limit[q : q + 1]
            piece = jnp.where(within, piece, 0.0).T
            high, low = split(piece)
            high_ref[q * 128 : (q + 1) * 128, b * 128 : (b + 1) * 128] = high
            low_ref[q * 128 : (q + 1) * 128, b * 128 : (b + 1) * 128] = low


def back_kernel(in_ref, high_ref, low_ref, out_ref, sum_s):
    for lat in range(N_LAT):
        total = in_ref[lat * 32 : lat * 32 + 8, :]
        for part in range(1, 4):
            total = total + in_ref[lat * 32 + part * 8 : lat * 32 + part * 8 + 8, :]
        sum_s[lat * 8 : lat * 8 + 8, :] = total
    lane = iota((16, 128), 1)
    for pair in range(2):
        rows = []
        for half in range(2):
            q = pair * 2 + half
            x = sum_s[pl.ds(q, 16, stride=8), :] + sum_s[pl.ds(q + 4, 16, stride=8), :]
            for u in range(4):
                for part in range(ROWS_DEV):
                    shift = ((half - part) * 16) % 128
                    moved = x if shift == 0 else pltpu.roll(x, shift, 1)
                    at = u * 32 + half * 16
                    rows.append(jnp.where((lane >= at) & (lane < at + 16), moved, 0.0))
        first = jnp.concatenate(rows[:8], axis=0).T
        second = jnp.concatenate(rows[8:], axis=0).T
        high, low = split(jnp.concatenate([first, second], axis=1))
        left = jnp.concatenate([high, low], axis=0)
        for b in range(MW // 256):
            lanes = slice(b * 256, (b + 1) * 256)
            both = dot(left, high_ref[pair * 256 : (pair + 1) * 256, lanes])
            value = both[:128] + both[128:]
            value = value + dot(high, low_ref[pair * 256 : (pair + 1) * 256, lanes])
            for s in range(8):
                slot = pair * 8 + s
                if slot >= PER_DEV:
                    continue
                for part in range(2):
                    for t in range(2):
                        at = (slot * 8 * 10 + b * 2 + t) * 2 + part
                        out_ref[pl.ds(at, 8, stride=20), :] = value[
                            s * 16 + part * 8 : s * 16 + part * 8 + 8, t * 128 : (t + 1) * 128
                        ]


diffusivity = 1.66
scatter_share = 0.2
heat_gain = 10.0


def shards(
    grid_fields, sun_cosine, surface_albedo, gas_absorb, solar_weight, helper_map, row_lat, wave_owner
):
    vmem = pl.BlockSpec(memory_space=pltpu.VMEM)
    smem = pl.BlockSpec(memory_space=pltpu.SMEM)
    outgoing, waves = pl.pallas_call(
        front_kernel,
        out_shape=(
            jax.ShapeDtypeStruct((DESTS * 4, 128), f32),
            jax.ShapeDtypeStruct((16, 128), f32),
        ),
        in_specs=[vmem, vmem, vmem, vmem, vmem, smem, smem, vmem],
        out_specs=(vmem, vmem),
        scratch_shapes=[
            pltpu.VMEM((128, 128), f32),
            pltpu.VMEM((128, 128), f32),
            pltpu.VMEM((ROWS_DEV, SEG_BLOCKS * 8, 128), f32),
            pltpu.VMEM((128, 512), f32),
        ],
        cost_estimate=pl.CostEstimate(flops=2 * 10**8, bytes_accessed=10**6, transcendentals=10**6),
        name="front",
    )(
        grid_fields,
        sun_cosine,
        surface_albedo,
        gas_absorb.reshape(1, G),
        solar_weight.reshape(1, G),
        helper_map,
        row_lat,
        wave_owner.reshape(1, MW),
    )
    incoming = lax.all_to_all(
        outgoing.reshape(DESTS, 4, 128), ("lat", "lon"), split_axis=0, concat_axis=0, tiled=True
    )
    high, low = pl.pallas_call(
        recur_kernel,
        out_shape=(
            jax.ShapeDtypeStruct((512, MW), bf16),
            jax.ShapeDtypeStruct((512, MW), bf16),
        ),
        in_specs=[vmem, smem],
        out_specs=(vmem, vmem),
        scratch_shapes=[pltpu.VMEM((MW * 4, 128), f32)],
        cost_estimate=pl.CostEstimate(flops=2 * 10**7, bytes_accessed=3 * 10**6, transcendentals=10**6),
        name="recur",
    )(waves, row_lat)
    rows = pl.pallas_call(
        back_kernel,
        out_shape=jax.ShapeDtypeStruct((PER_DEV * K * 10 * 2, 128), f32),
        in_specs=[vmem, vmem, vmem],
        out_specs=vmem,
        scratch_shapes=[pltpu.VMEM((128, 128), f32)],
        cost_estimate=pl.CostEstimate(flops=5 * 10**8, bytes_accessed=4 * 10**6, transcendentals=0),
        name="back",
    )(incoming.reshape(DESTS * 4, 128), high, low)
    return (
        rows.reshape(PER_DEV, K, 10, 2, 128).transpose(0, 1, 3, 2, 4).reshape(PER_DEV, K, 2, MW)
    )


def solution(mesh):
    placed = (
        P(None, "lat", "lon"),
        P("lat", "lon"),
        P("lat", "lon"),
        P(),
        P(),
        P("lat", "lon"),
        P(),
        P(),
    )
    return jax.shard_map(
        shards,
        mesh=mesh,
        in_specs=placed,
        out_specs=P(("lat", "lon"), None, None, None),
        check_vma=False,
    )
```

time: 1520 us -> 40.6 us (0.03); the launches traced: 1500 us -> 40.2 us
  local copies, waits for them, and re-layouts: 1250 us -> 5.41 us
  other arithmetic: 163 us -> 0 us
  matrix products: 40 us -> 0 us
  loops' own time: 21.8 us -> 0 us
  Pallas kernels: 0 us -> 19.5 us
    another operation x1300 -> x0, local copies, waits for them, and re-layouts: 1210 us -> none  [one_turn(): stacked = jnp.stack(rows_out, axis=1)]
    another operation x140 -> x0, other arithmetic: 94.5 us -> none  [one_turn(): stacked = jnp.stack(rows_out, axis=1)]
    dot_general x21 -> x0, matrix products: 40 us -> none  [the longest x20 37.7 us: one_turn(): contrib = jnp.einsum('skr,scr->sck', stacked, inputs, precision=highest)]
    sqrt x81 -> x0, other arithmetic: 22.1 us -> none  [the longest x80 21.6 us: advance(): factor_a = jnp.sqrt((4.0 * degree * degree - 1.0) / square)]
    another operation x2 -> x0, loops' own time: 21.8 us -> none  [the longest x1 21.6 us: legendre(): lax.scan(one_turn, (jnp.zeros_like(start_vals), start_vals), jnp.arange(t...]
    pallas_call x0 -> x3, Pallas kernels: none -> 19.5 us  [the longest x1 8.86 us: shards(): pl.pallas_call(front_kernel, out_shape=(jax.ShapeDtypeStruct((DESTS * 4,...]
    cos x2 -> x0, other arithmetic: 18.6 us -> none  [the longest x1 17.9 us: inner_table(): return jnp.concatenate([jnp.cos(angles), -jnp.sin(angles)], axis=1)]
  transfers between devices with their start and end apart: 2 -> 1, of which waited for: 1 -> 1; matrix products, arithmetic and copies ran while one was open for 2% -> 0% of each run, Pallas kernels for 0% -> 17%
where the time goes in v1:
time: 40.6 us; the launch traced here: 40.2 us
  Pallas kernels  19.5 us (48%)
  starting transfers between devices  11.5 us (28%)
  local copies, waits for them, and re-layouts  5.41 us (13%)
  waiting for transfers between devices  3.78 us (9%)
    all_to_all x1, starting transfers between devices, shards(): lax.all_to_all(outgoing.reshape(DESTS, 4, 128), ('lat', 'lon'), split_axi...  11.5 us
    pallas_call x1, Pallas kernels, shards(): pl.pallas_call(front_kernel, out_shape=(jax.ShapeDtypeStruct((DESTS * 4,...  8.86 us
    pallas_call x1, Pallas kernels, shards(): pl.pallas_call(recur_kernel, out_shape=(jax.ShapeDtypeStruct((512, MW), b...  7.02 us
    all_to_all x1, waiting for transfers between devices, shards(): lax.all_to_all(outgoing.reshape(DESTS, 4, 128), ('lat', 'lon'), split_axi...  3.78 us
    pallas_call x1, Pallas kernels, shards(): pl.pallas_call(back_kernel, out_shape=jax.ShapeDtypeStruct((PER_DEV * K *...  3.63 us
    reshape x3, local copies, waits for them, and re-layouts, shards(): rows.reshape(PER_DEV, K, 10, 2, 128).transpose(0, 1, 3, 2, 4)  3.42 us
    reshape x1, local copies, waits for them, and re-layouts, shards(): wave_owner.reshape(1, MW)  1.29 us
  transfers between devices with their start and end apart: 1, of which 1 were waited for; matrix products, arithmetic and copies ran while one was open for 0% of the time, Pallas kernels for 17%

profile of v1, /device:TPU:1, one launch (start us, length us, event | category | flops | bytes accessed | tf_op | source)
XLA Modules:
  0.0 40.2 jit_solution(10675973983434791977)
XLA Ops:
  0.0 1.3 %reshape.23.owner_ref = s32[1,1280]{1,0:T(1,128)} reshape(s32[1280]{0:T(1024)} %param.15) | data formatting | bytes 10240 | tf_op jit(solution)/shard_map/reshape | solution.py:398
  1.3 8.9 %front.1 = (f32[512,128]{1,0:T(8,128)}, f32[16,128]{1,0:T(8,128)}) custom-call(f32[8,2,768]{2,1,0:T(2,128)} %fields_ref.1, f32[2,768]{1,0:T(2,128)} %sun_ref.1, f32[2,768]{1,0:T(2,128)} %ground_ref.1, f32[1,112]{1,0:T(1,128)} %bitcast.14, f32[1,112]{1,0:T(1,128)} %bitcast.15, s32[2,6]{1,0:T(2,128)} %lit_ref.1, s32[32]{0:T(128)} %row_ref.3, ...), custom_call_target="tpu_custom_call" | custom-call | flops 200000000 | bytes 1000000 | tf_op jit(solution)/shard_map/front/pallas_call | solution.py:374
  10.2 11.5 %all-to-all-start = ((f32[128,4,128]{2,1,0:T(4,128)}), f32[128,4,128]{2,1,0:T(4,128)S(1)}, u32[]{:S(2)}, u32[]{:S(2)}) async-start(f32[128,4,128]{2,1,0:T(4,128)} %bitcast.13), calls=%async_computation | async-start | bytes 524288 | tf_op jit(solution)/shard_map/all_to_all | solution.py:400
  21.6 7.0 %recur.1 = (bf16[512,1280]{1,0:T(8,128)(2,1)}, bf16[512,1280]{1,0:T(8,128)(2,1)}) custom-call(f32[16,128]{1,0:T(8,128)} %get-tuple-element.10.wave_ref, s32[32]{0:T(128)} %row_ref.3), custom_call_target="tpu_custom_call" | custom-call | flops 20000000 | bytes 3000000 | tf_op jit(solution)/shard_map/recur/pallas_call | solution.py:403
  28.7 3.8 %all-to-all-done = f32[128,4,128]{2,1,0:T(4,128)S(1)} async-done(((f32[128,4,128]{2,1,0:T(4,128)}), f32[128,4,128]{2,1,0:T(4,128)S(1)}, u32[]{:S(2)}, u32[]{:S(2)}) %all-to-all-start) | async-done | bytes 262176 | tf_op jit(solution)/shard_map/all_to_all | solution.py:400
  32.4 0.0 copy-start
  32.5 0.7 %copy-done = f32[128,4,128]{2,1,0:T(4,128)} copy-done((f32[128,4,128]{2,1,0:T(4,128)}, f32[128,4,128]{2,1,0:T(4,128)S(1)}, u32[]{:S(2)}) %copy-start) | copy-done | bytes 262168
  33.1 3.6 %back.1 = f32[2400,128]{1,0:T(8,128)} custom-call(f32[512,128]{1,0:T(8,128)} %bitcast.12, bf16[512,1280]{1,0:T(8,128)(2,1)} %get-tuple-element.11.high_ref, bf16[512,1280]{1,0:T(8,128)(2,1)} %get-tuple-element.12.low_ref), custom_call_target="tpu_custom_call" | custom-call | flops 500000000 | bytes 4000000 | tf_op jit(solution)/shard_map/back/pallas_call | solution.py:415
  36.8 1.5 %copy.13 = f32[15,8,10,2,128]{4,2,1,3,0:T(8,128)S(1)} copy(f32[15,8,10,2,128]{4,3,2,1,0:T(2,128)} %bitcast.11) | data formatting | bytes 2457600 | tf_op jit(solution)/shard_map/reshape | solution.py:425
  38.3 0.2 reshape.27
  38.5 1.7 %copy.11 = f32[15,8,2,1280]{3,2,1,0:T(2,128)} copy(f32[15,8,2,1280]{3,1,2,0:T(8,128)S(1)} %reshape.27) | data formatting | bytes 2457600 | tf_op jit(solution)/shard_map/reshape | solution.py:425
Async XLA Ops:
  10.2 22.3 %all-to-all-start = ((f32[128,4,128]{2,1,0:T(4,128)}), f32[128,4,128]{2,1,0:T(4,128)S(1)}, u32[]{:S(2)}, u32[]{:S(2)}) async-start(f32[128,4,128]{2,1,0:T(4,128)} %bitcast.13), calls=%async_computation | async-start | bytes 524288 | tf_op jit(solution)/shard_map/all_to_all | solution.py:400
  32.4 0.7 %copy-start = (f32[128,4,128]{2,1,0:T(4,128)}, f32[128,4,128]{2,1,0:T(4,128)S(1)}, u32[]{:S(2)}) copy-start(f32[128,4,128]{2,1,0:T(4,128)S(1)} %all-to-all-done) | copy-start | bytes 786436

commit v2 on v1

v2 whole, which is shorter than its diff:
```python
import math

import jax
import jax.numpy as jnp
from jax import lax
from jax.experimental import pallas as pl
from jax.experimental.pallas import tpu as pltpu
from jax.sharding import PartitionSpec as P

LEV = 4
BLOCK = 128
NLAT_FULL = 2560
MW = 1280
G = 112
K = 8
SEG_BLOCKS = 6
ROWS_DEV = 2
N_LAT = 16
N_LON = 8
DESTS = N_LAT * N_LON
PER_DEV = 15
MCAP = PER_DEV * N_LON
ROWS_T = N_LAT * ROWS_DEV
LOG2E = math.log2(math.e)

f32 = jnp.float32
bf16 = jnp.bfloat16


def iota(shape, dim):
    return lax.broadcasted_iota(jnp.int32, shape, dim)


def dot(a, b, contract=(1, 0)):
    return lax.dot_general(
        a, b, (((contract[0],), (contract[1],)), ((), ())), preferred_element_type=f32
    )


def split(x):
    high = x.astype(bf16)
    return high, (x - high.astype(f32)).astype(bf16)


def sincos_quarter(r):
    r2 = r * r
    sin_v = r + (r * r2) * (-1.6666654611e-1 + r2 * (8.3321608736e-3 - r2 * 1.9515295891e-4))
    cos_v = 1.0 + r2 * (
        -0.5 + r2 * (4.166664568298827e-2 + r2 * (-1.388731625493765e-3 + r2 * 2.443315711809948e-5))
    )
    for _ in range(2):
        twice = sin_v + sin_v
        cos_v, sin_v = 1.0 - twice * sin_v, twice * cos_v
    return cos_v, sin_v


def slot_of(lane_q, lane_u):
    return (lane_q // 2) * 8 + lane_u * 2 + lane_q % 2


def slot_picks(pick_ref):
    lane = iota((128, 128), 1)
    for u in range(4):
        index = slot_of(lane % 4, u)
        rank = ((lane // 4) % N_LON) * PER_DEV + index
        pick = (iota((128, 128), 0) == rank) & (index < PER_DEV)
        pick_ref[u] = pick.astype(f32).astype(bf16)


def find_slots(owner_ref, pick_ref, wave_ref):
    groups = MW // 128
    hits = [
        (owner_ref[b : b + 1, :] == iota((N_LAT, 128), 0)).astype(f32) for b in range(groups)
    ]
    stacked = jnp.concatenate(hits, axis=0).astype(bf16)
    before = (iota((128, 128), 0) < iota((128, 128), 1)).astype(f32).astype(bf16)
    ahead = dot(stacked, before)
    total = dot(stacked, jnp.ones((128, 128), bf16))
    carry = jnp.zeros((N_LAT, 128), f32)
    table = jnp.zeros((2 * N_LAT, 128), f32)
    for b in range(groups):
        part = slice(b * N_LAT, (b + 1) * N_LAT)
        rank = jnp.sum(hits[b] * (ahead[part] + carry), axis=0, keepdims=True)
        carry = carry + total[part]
        ranked = (rank.astype(jnp.int32) == iota((128, 128), 0)).astype(f32).astype(bf16)
        number = iota((N_LAT, 128), 1) + (b * 128 + 1)
        high = ((number >> 4) << 4).astype(f32)
        low = (number & 15).astype(f32)
        both = jnp.concatenate([hits[b] * high, hits[b] * low], axis=0).astype(bf16)
        table = table + dot(both, ranked, (1, 1))
    table = table.astype(bf16)
    for u in range(4):
        found = dot(table, pick_ref[u])
        found = found[:N_LAT] + found[N_LAT:]
        for g in range(4):
            own = iota((N_LAT, 128), 0) == g * 4 + iota((N_LAT, 128), 1) // 32
            wave_ref[u * 4 + g : u * 4 + g + 1, :] = jnp.sum(
                jnp.where(own, found, 0.0), axis=0, keepdims=True
            )


def front_kernel(
    fields_hbm, sun_hbm, ground_hbm, gas_hbm, weight_hbm, lit_hbm, row_hbm, owner_hbm,
    out_hbm, wave_ref,
    fields_ref, sun_ref, ground_ref, gas_ref, weight_ref, lit_ref, row_ref, owner_ref,
    out_s, pick_s, gas_s, weight_s, left_s, spec_s, turn_s, in_sems, out_sems,
):
    lat_me = lax.axis_index("lat")
    lon_me = lax.axis_index("lon")
    pairs = [
        (owner_hbm, owner_ref),
        (gas_hbm, gas_ref),
        (weight_hbm, weight_ref),
        (row_hbm, row_ref),
        (lit_hbm, lit_ref),
        (sun_hbm, sun_ref),
        (ground_hbm, ground_ref),
    ] + [(fields_hbm.at[:, g, :], fields_ref.at[g]) for g in range(ROWS_DEV)]
    arrivals = [
        pltpu.make_async_copy(source, target, in_sems.at[index])
        for index, (source, target) in enumerate(pairs)
    ]
    for copy in arrivals:
        copy.start()
    slot_picks(pick_s)
    arrivals[0].wait()
    find_slots(owner_ref, pick_s, wave_ref)
    for copy in arrivals[1:]:
        copy.wait()

    def column(row):
        padded = jnp.concatenate([row, jnp.zeros((1, 128 - G), f32)], axis=1)
        return jnp.broadcast_to(padded, (128, 128)).T

    total_weight = jnp.sum(weight_ref[...], axis=1, keepdims=True)
    gas_s[...] = column(gas_ref[...])
    weight_s[...] = column(weight_ref[...] * (heat_gain / total_weight))

    counts = []
    for g in range(ROWS_DEV):
        row = row_ref[lat_me * ROWS_DEV + g]
        counts.append(20 + 4 * jnp.minimum(row, NLAT_FULL - 1 - row))

    for g in range(ROWS_DEV):

        def heat_block(a, carry, g=g):
            columns = pl.ds(pl.multiple_of(a * BLOCK, BLOCK), BLOCK)
            x = fields_ref[g, :, columns]
            depth = jnp.maximum(x, 0.0) + jnp.log1p(jnp.exp(-jnp.abs(x)))
            sun = sun_ref[g : g + 1, columns]
            slant = depth * (-LOG2E / sun)
            diffuse = depth * (-LOG2E * diffusivity)
            tile = lambda row: jnp.broadcast_to(row, (8, BLOCK))
            sun_b = tile(sun * scatter_share)
            ground = ground_ref[g : g + 1, columns]
            ground_b = tile(ground)
            slants = [tile(slant[level : level + 1]) for level in range(LEV)]
            diffuses = [tile(diffuse[level : level + 1]) for level in range(LEV)]
            nets = [jnp.zeros((8, BLOCK), f32) for _ in range(LEV + 1)]
            beams = [jnp.zeros((8, BLOCK), f32) for _ in range(LEV + 1)]
            for part in range(G // 8):
                gas = gas_s[part * 8 : (part + 1) * 8, :]
                beam = sun_b * weight_s[part * 8 : (part + 1) * 8, :]
                beams[0] = beams[0] + beam
                down, downs, sources, passed = None, [], [], []
                for level in range(LEV):
                    after = beam * jnp.exp2(gas * slants[level])
                    source = beam - after
                    beam = after
                    t_dif = jnp.exp2(gas * diffuses[level])
                    down = source if down is None else down * t_dif + source
                    beams[level + 1] = beams[level + 1] + beam
                    downs.append(down)
                    sources.append(source)
                    passed.append(t_dif)
                nets[LEV] = nets[LEV] + down
                upward = ground_b * (beam * (1.0 / scatter_share) + down)
                for level in range(LEV - 1, -1, -1):
                    upward = upward * passed[level] + sources[level]
                    if level:
                        nets[level] = nets[level] + (downs[level - 1] - upward)
                    else:
                        nets[level] = nets[level] - upward
            nets = [net + beams[level] * (1.0 / scatter_share) for level, net in enumerate(nets)]
            nets[LEV] = nets[LEV] * (1.0 - ground)
            sums = [nets[level] - nets[level + 1] for level in range(LEV)]
            is_lit = lit_ref[g, a] >= 0
            heated = x
            for level in range(LEV):
                heat = jnp.where(is_lit, jnp.sum(sums[level], axis=0, keepdims=True), 0.0)
                heated = heated + jnp.where(iota((8, BLOCK), 0) == LEV + level, heat, 0.0)
            first = (lon_me * SEG_BLOCKS + a) * BLOCK
            heated = jnp.where(iota((8, BLOCK), 1) + first < counts[g], heated, 0.0)
            left_s[g, pl.ds(pl.multiple_of(a * 8, 8), 8), :] = heated
            return carry

        lax.fori_loop(0, SEG_BLOCKS, heat_block, 0)

    offset, place = iota((BLOCK, BLOCK), 0), iota((BLOCK, BLOCK), 1)
    half = BLOCK // 2
    step = place % half
    fold = jnp.where(offset == half + step, 1.0, 0.0)
    mirror = jnp.where(offset == half - 1 - step, 1.0, 0.0)
    fold = (fold + jnp.where(place < half, mirror, -mirror)).astype(bf16)
    size = SEG_BLOCKS * 8
    is_even = iota((size, BLOCK), 1) < half
    lefts = []
    for g in range(ROWS_DEV):
        x = left_s[g]
        first = x.astype(bf16)
        second, third = split(x - first.astype(f32))
        folded = dot(jnp.concatenate([first, second, third], axis=0), fold)
        folded = folded[:size] + (folded[size : 2 * size] + folded[2 * size :])
        evens = split(jnp.where(is_even, folded, 0.0))
        odds = split(jnp.where(is_even, 0.0, folded))
        empty = jnp.zeros((size, BLOCK), bf16)
        lefts.append(
            jnp.concatenate(
                [
                    jnp.concatenate([evens[0], evens[0]], axis=1),
                    jnp.concatenate([odds[0], odds[0]], axis=1),
                    jnp.concatenate([evens[1], empty], axis=1),
                    jnp.concatenate([odds[1], empty], axis=1),
                ],
                axis=0,
            )
        )

    sub = iota((8, 128), 0)
    first_block = (lon_me * SEG_BLOCKS * 2 * BLOCK).astype(f32)
    steps = jnp.concatenate(
        [
            (sub * 2 + 1).astype(f32),
            (sub * 16).astype(f32),
            (sub * (2 * BLOCK) + (BLOCK - 1)).astype(f32) + first_block,
        ],
        axis=0,
    )
    steps = jnp.where(iota((24, 128), 0) < 16 + SEG_BLOCKS, steps, 0.0)
    departures = []
    for lat_group in range(4):
        lanes = slice(lat_group * 128, (lat_group + 1) * 128)
        for pair in range(2):
            for g in range(ROWS_DEV):
                n = jnp.full((1, 128), counts[g] * 2, jnp.int32).astype(f32)
                inverse = 1.0 / n
                scale = lax.rsqrt(n * (ROWS_T / 2))
                rights = []
                for u in (pair * 2, pair * 2 + 1):
                    index = u * 4 + lat_group
                    wave = jnp.maximum(wave_ref[index : index + 1, :] - 1.0, 0.0)
                    phase = steps * wave
                    phase = phase - n * jnp.round(phase * inverse)
                    cos_v, sin_v = sincos_quarter(phase * (inverse * (math.pi / 2)))
                    at = (g * 16 + index) * 32
                    turn_s[at : at + 8, :] = cos_v[8:16]
                    turn_s[at + 8 : at + 16, :] = sin_v[8:16]
                    turn_s[at + 16 : at + 24, :] = cos_v[16:] * scale
                    turn_s[at + 24 : at + 32, :] = sin_v[16:] * scale
                    cos_low, sin_low = cos_v[:8], sin_v[:8]
                    cos_h, cos_l, sin_h, sin_l = [], [], [], []
                    for b in range(0, 8, 2):
                        cos_p, sin_p = [], []
                        for r in (b, b + 1):
                            cos_r = turn_s[pl.ds(at + r, 8, stride=0), :]
                            sin_r = turn_s[pl.ds(at + 8 + r, 8, stride=0), :]
                            cos_p.append(cos_low * cos_r - sin_low * sin_r)
                            sin_p.append(sin_low * cos_r + cos_low * sin_r)
                        high, low = split(jnp.concatenate(cos_p, axis=0))
                        cos_h.append(high)
                        cos_l.append(low)
                        high, low = split(jnp.concatenate(sin_p, axis=0))
                        sin_h.append(high)
                        sin_l.append(low)
                    rights.append(jnp.concatenate(cos_h + sin_h + cos_l + sin_l, axis=0))
                both = dot(lefts[g], jnp.concatenate(rights, axis=1))
                both = both[: 2 * size] + both[2 * size :]
                for k in range(2):
                    u = pair * 2 + k
                    at = (g * 16 + u * 4 + lat_group) * 32
                    real = jnp.zeros((8, 128), f32)
                    imag = jnp.zeros((8, 128), f32)
                    for a in range(SEG_BLOCKS):
                        c = both[a * 8 : a * 8 + 8, k * 128 : (k + 1) * 128]
                        s = both[size + a * 8 : size + a * 8 + 8, k * 128 : (k + 1) * 128]
                        cos_a = turn_s[pl.ds(at + 16 + a, 8, stride=0), :]
                        sin_a = turn_s[pl.ds(at + 24 + a, 8, stride=0), :]
                        real = real + (cos_a * c - sin_a * s)
                        imag = imag - (cos_a * s + sin_a * c)
                    row = u * 32 + g * 16
                    spec_s[row : row + 16, lanes] = jnp.concatenate([real, imag], axis=0)
        out_s[lanes, :] = spec_s[:, lanes].T
        copy = pltpu.make_async_copy(out_s.at[lanes, :], out_hbm.at[lanes, :], out_sems.at[lat_group])
        copy.start()
        departures.append(copy)
    for copy in departures:
        copy.wait()


def recur_kernel(wave_ref, row_ref, high_ref, low_ref, poly_s):
    lat_me = lax.axis_index("lat")
    lon_me = lax.axis_index("lon")
    me = lat_me * N_LON + lon_me
    group = me // 32
    lane = iota((1, 128), 1)
    rows = jnp.zeros((1, 128), jnp.int32)
    for part in range(ROWS_DEV):
        for lat in range(N_LAT):
            rows = jnp.where(lane % 32 == part * 16 + lat, row_ref[lat * 2 + part], rows)
    angle = (NLAT_FULL / 2 - 0.5) - rows.astype(f32)
    _, x = sincos_quarter(jnp.broadcast_to(angle * (math.pi / (4 * NLAT_FULL)), (4, 128)))
    log_sin = 0.5 * jnp.log1p(-x * x)

    found = []
    for q in range(4):
        total = jnp.zeros((1, 128), f32)
        for u in range(4):
            mine = wave_ref[pl.ds(u * 4 + group, 1), :]
            value = jnp.sum(
                jnp.where(lane == (me % 32) * 4 + q, mine, 0.0), axis=1, keepdims=True
            )
            total = jnp.where(lane // 32 == u, value, total)
        found.append(total)
    number = jnp.concatenate(found, axis=0)
    m = jnp.maximum(number - 1.0, 0.0)
    limit = jnp.where(number > 0.5, MW - m, 0.0)

    z = m + 1.0
    ratio = (z * (z + 1.0) * (z + 2.0) * (z + 3.0)) / (
        (z + 0.5) * (z + 1.5) * (z + 2.5) * (z + 3.5)
    )
    far = 1.0 / (z + 4.0)
    far2 = far * far
    log_ratio = (
        0.5 * jnp.log(z + 4.0)
        + far * (-1.0 / 8 + far2 * (1.0 / 192 - far2 * (1.0 / 640)))
        + jnp.log(ratio)
    )
    log_start = 0.5 * (
        log_ratio - math.lgamma(1.5) + jnp.where(m > 0.5, math.log(2.0), 0.0)
    )
    start = jnp.exp(log_start + m * log_sin)
    twice = 2.0 * m

    unroll = 16

    def turn(t, state):
        previous, current, shrink = state
        base = (t * unroll).astype(f32)
        for j in range(unroll):
            poly_s[pl.ds(pl.multiple_of(t * (unroll * 4), unroll * 4) + j * 4, 4), :] = current
            step = base + (j + 1.0)
            reach = twice + step
            degree2 = reach + step
            square = degree2 * degree2 - 1.0
            gap = step * reach
            root = lax.rsqrt(square * gap)
            grow = square * root
            previous, current = (
                current,
                (grow * x) * current - (grow * shrink) * previous,
            )
            shrink = gap * root
        return previous, current, shrink

    zero = jnp.zeros((4, 128), f32)
    lax.fori_loop(0, MW // unroll, turn, (zero, start, zero))

    for q in range(4):
        for b in range(MW // 128):
            piece = poly_s[pl.ds(b * 512 + q, 128, stride=4), :]
            within = (iota((128, 128), 0) + b * 128).astype(f32) < limit[q : q + 1]
            piece = jnp.where(within, piece, 0.0).T
            high, low = split(piece)
            high_ref[q * 128 : (q + 1) * 128, b * 128 : (b + 1) * 128] = high
            low_ref[q * 128 : (q + 1) * 128, b * 128 : (b + 1) * 128] = low


def back_kernel(in_ref, high_ref, low_ref, out_ref, sum_s, result_s, sems):
    for lat in range(N_LAT):
        total = in_ref[lat * 32 : lat * 32 + 8, :]
        for part in range(1, 4):
            total = total + in_ref[lat * 32 + part * 8 : lat * 32 + part * 8 + 8, :]
        sum_s[lat * 8 : lat * 8 + 8, :] = total
    lane = iota((16, 128), 1)
    lefts = []
    for pair in range(2):
        rows = []
        for half in range(2):
            q = pair * 2 + half
            x = sum_s[pl.ds(q, 16, stride=8), :] + sum_s[pl.ds(q + 4, 16, stride=8), :]
            for u in range(4):
                for part in range(ROWS_DEV):
                    shift = ((half - part) * 16) % 128
                    moved = x if shift == 0 else pltpu.roll(x, shift, 1)
                    at = u * 32 + half * 16
                    rows.append(jnp.where((lane >= at) & (lane < at + 16), moved, 0.0))
        first = jnp.concatenate(rows[:8], axis=0).T
        second = jnp.concatenate(rows[8:], axis=0).T
        lefts.append(split(jnp.concatenate([first, second], axis=1)))
    copies = []
    for b in range(MW // 256):
        lanes = slice(b * 256, (b + 1) * 256)
        for pair in range(2):
            high, low = lefts[pair]
            rows = slice(pair * 256, (pair + 1) * 256)
            both = dot(jnp.concatenate([high, low], axis=0), high_ref[rows, lanes])
            value = both[:128] + both[128:] + dot(high, low_ref[rows, lanes])
            for s in range(8):
                slot = pair * 8 + s
                if slot < PER_DEV:
                    for part in range(2):
                        at = s * 16 + part * 8
                        result_s[slot, :, part, lanes] = value[at : at + 8]
        copy = pltpu.make_async_copy(
            result_s.at[:, :, :, lanes], out_ref.at[:, :, :, lanes], sems.at[b]
        )
        copy.start()
        copies.append(copy)
    for copy in copies:
        copy.wait()


diffusivity = 1.66
scatter_share = 0.2
heat_gain = 10.0


def shards(
    grid_fields, sun_cosine, surface_albedo, gas_absorb, solar_weight, helper_map, row_lat, wave_owner
):
    vmem = pl.BlockSpec(memory_space=pltpu.VMEM)
    smem = pl.BlockSpec(memory_space=pltpu.SMEM)
    hbm = pl.BlockSpec(memory_space=pl.ANY)
    limits = pltpu.CompilerParams(vmem_limit_bytes=16 * 2**20)
    outgoing, waves = pl.pallas_call(
        front_kernel,
        out_shape=(
            jax.ShapeDtypeStruct((DESTS * 4, 128), f32),
            jax.ShapeDtypeStruct((16, 128), f32),
        ),
        in_specs=[hbm] * 8,
        out_specs=(hbm, vmem),
        scratch_shapes=[
            pltpu.VMEM((ROWS_DEV, K, SEG_BLOCKS * BLOCK), f32),
            pltpu.VMEM((ROWS_DEV, SEG_BLOCKS * BLOCK), f32),
            pltpu.VMEM((ROWS_DEV, SEG_BLOCKS * BLOCK), f32),
            pltpu.VMEM((1, G), f32),
            pltpu.VMEM((1, G), f32),
            pltpu.SMEM((ROWS_DEV, SEG_BLOCKS), jnp.int32),
            pltpu.SMEM((ROWS_T,), jnp.int32),
            pltpu.VMEM((MW // 128, 128), jnp.int32),
            pltpu.VMEM((DESTS * 4, 128), f32),
            pltpu.VMEM((4, 128, 128), bf16),
            pltpu.VMEM((128, 128), f32),
            pltpu.VMEM((128, 128), f32),
            pltpu.VMEM((ROWS_DEV, SEG_BLOCKS * 8, 128), f32),
            pltpu.VMEM((128, 512), f32),
            pltpu.VMEM((1024, 128), f32),
            pltpu.SemaphoreType.DMA((9,)),
            pltpu.SemaphoreType.DMA((4,)),
        ],
        cost_estimate=pl.CostEstimate(flops=2 * 10**8, bytes_accessed=10**6, transcendentals=10**6),
        name="front",
        compiler_params=pltpu.CompilerParams(vmem_limit_bytes=60 * 2**20),
    )(
        grid_fields,
        sun_cosine,
        surface_albedo,
        gas_absorb.reshape(1, G),
        solar_weight.reshape(1, G),
        helper_map,
        row_lat,
        wave_owner.reshape(MW // 128, 128),
    )
    incoming = lax.all_to_all(
        outgoing.reshape(DESTS, 4, 128), ("lat", "lon"), split_axis=0, concat_axis=0, tiled=True
    )
    high, low = pl.pallas_call(
        recur_kernel,
        out_shape=(
            jax.ShapeDtypeStruct((512, MW), bf16),
            jax.ShapeDtypeStruct((512, MW), bf16),
        ),
        in_specs=[vmem, smem],
        out_specs=(vmem, vmem),
        scratch_shapes=[pltpu.VMEM((MW * 4, 128), f32)],
        cost_estimate=pl.CostEstimate(flops=2 * 10**7, bytes_accessed=3 * 10**6, transcendentals=10**6),
        name="recur",
        compiler_params=limits,
    )(waves, row_lat)
    return pl.pallas_call(
        back_kernel,
        out_shape=jax.ShapeDtypeStruct((PER_DEV, K, 2, MW), f32),
        in_specs=[vmem, vmem, vmem],
        out_specs=pl.BlockSpec(memory_space=pl.ANY),
        scratch_shapes=[
            pltpu.VMEM((128, 128), f32),
            pltpu.VMEM((PER_DEV, K, 2, MW), f32),
            pltpu.SemaphoreType.DMA((MW // 256,)),
        ],
        cost_estimate=pl.CostEstimate(flops=5 * 10**8, bytes_accessed=4 * 10**6, transcendentals=0),
        name="back",
        compiler_params=limits,
    )(incoming.reshape(DESTS * 4, 128), high, low)


def solution(mesh):
    placed = (
        P(None, "lat", "lon"),
        P("lat", "lon"),
        P("lat", "lon"),
        P(),
        P(),
        P("lat", "lon"),
        P(),
        P(),
    )
    return jax.shard_map(
        shards,
        mesh=mesh,
        in_specs=placed,
        out_specs=P(("lat", "lon"), None, None, None),
        check_vma=False,
    )
```

time: 40.6 us -> 30.4 us (0.75)
  Pallas kernels: 19.5 us -> 13.1 us
  local copies, waits for them, and re-layouts: 5.41 us -> 0.69 us
  waiting for transfers between devices: 3.78 us -> 4.82 us
    reshape x4 -> x0, local copies, waits for them, and re-layouts: 4.71 us -> none  [the longest x3 3.42 us: shards(): rows.reshape(PER_DEV, K, 10, 2, 128).transpose(0, 1, 3, 2, 4)]
    pallas_call x1, Pallas kernels: 8.86 us -> 6.22 us  [shards(): pl.pallas_call(front_kernel, out_shape=(jax.ShapeDtypeStruct((DESTS * 4,...]
    pallas_call x1, Pallas kernels: 3.63 us -> 1.66 us  [shards(): pl.pallas_call(back_kernel, out_shape=jax.ShapeDtypeStruct((PER_DEV, K, 2...]
    pallas_call x1, Pallas kernels: 7.02 us -> 5.27 us  [shards(): pl.pallas_call(recur_kernel, out_shape=(jax.ShapeDtypeStruct((512, MW), b...]
    all_to_all x1, waiting for transfers between devices: 3.78 us -> 4.82 us  [shards(): lax.all_to_all(outgoing.reshape(DESTS, 4, 128), ('lat', 'lon'), split_axi...]
where the time goes in v2:
time: 30.4 us; the launch traced here: 30.2 us
  Pallas kernels  13.1 us (43%)
  starting transfers between devices  11.5 us (38%)
  waiting for transfers between devices  4.82 us (16%)
  local copies, waits for them, and re-layouts  0.69 us (2%)
    all_to_all x1, starting transfers between devices, shards(): lax.all_to_all(outgoing.reshape(DESTS, 4, 128), ('lat', 'lon'), split_axi...  11.5 us
    pallas_call x1, Pallas kernels, shards(): pl.pallas_call(front_kernel, out_shape=(jax.ShapeDtypeStruct((DESTS * 4,...  6.22 us
    pallas_call x1, Pallas kernels, shards(): pl.pallas_call(recur_kernel, out_shape=(jax.ShapeDtypeStruct((512, MW), b...  5.27 us
    all_to_all x1, waiting for transfers between devices, shards(): lax.all_to_all(outgoing.reshape(DESTS, 4, 128), ('lat', 'lon'), split_axi...  4.82 us
    pallas_call x1, Pallas kernels, shards(): pl.pallas_call(back_kernel, out_shape=jax.ShapeDtypeStruct((PER_DEV, K, 2...  1.66 us
    unnamed x4, local copies, waits for them, and re-layouts  0.69 us
  transfers between devices with their start and end apart: 1, of which 1 were waited for; matrix products, arithmetic and copies ran while one was open for 0% of the time, Pallas kernels for 17%

profile of v2, /device:TPU:1, one launch (start us, length us, event | category | flops | bytes accessed | tf_op | source)
XLA Modules:
  0.0 30.2 jit_solution(773972513744783010)
XLA Ops:
  0.0 0.0 copy-start
  0.0 6.2 %front.1 = (f32[512,128]{1,0:T(8,128)}, f32[16,128]{1,0:T(8,128)}) custom-call(f32[8,2,768]{2,1,0:T(2,128)} %fields_hbm.1, f32[2,768]{1,0:T(2,128)} %sun_hbm.1, f32[2,768]{1,0:T(2,128)} %ground_hbm.1, f32[1,112]{1,0:T(1,128)} %bitcast.8, f32[1,112]{1,0:T(1,128)} %bitcast.9, s32[2,6]{1,0:T(2,128)} %lit_hbm.1, s32[32]{0:T(128)} %row_ref.1, s32[10,128]{1,0:T(8,128)} %bitcast.7), custom_call_target="tpu_custom_call" | custom-call | flops 200000000 | bytes 1000000 | tf_op jit(solution)/shard_map/front/pallas_call | solution.py:436
  6.2 11.5 %all-to-all-start = ((f32[128,4,128]{2,1,0:T(4,128)}), f32[128,4,128]{2,1,0:T(4,128)S(1)}, u32[]{:S(2)}, u32[]{:S(2)}) async-start(f32[128,4,128]{2,1,0:T(4,128)} %bitcast.6), calls=%async_computation | async-start | bytes 524288 | tf_op jit(solution)/shard_map/all_to_all | solution.py:476
  17.7 0.0 copy-done
  17.7 0.0 copy-start.1
  17.8 0.7 %copy-done.1 = f32[16,128]{1,0:T(8,128)S(1)} copy-done((f32[16,128]{1,0:T(8,128)S(1)}, f32[16,128]{1,0:T(8,128)}, u32[]{:S(2)}) %copy-start.1) | copy-done | bytes 8216
  18.4 5.3 %recur.1 = (bf16[512,1280]{1,0:T(8,128)(2,1)S(1)}, bf16[512,1280]{1,0:T(8,128)(2,1)S(1)}) custom-call(f32[16,128]{1,0:T(8,128)S(1)} %copy-done.1, s32[32]{0:T(128)S(1)} %copy-done), custom_call_target="tpu_custom_call" | custom-call | flops 20000000 | bytes 3000000 | tf_op jit(solution)/shard_map/recur/pallas_call | solution.py:479
  23.7 4.8 %all-to-all-done = f32[128,4,128]{2,1,0:T(4,128)S(1)} async-done(((f32[128,4,128]{2,1,0:T(4,128)}), f32[128,4,128]{2,1,0:T(4,128)S(1)}, u32[]{:S(2)}, u32[]{:S(2)}) %all-to-all-start) | async-done | bytes 262176 | tf_op jit(solution)/shard_map/all_to_all | solution.py:476
  28.5 1.7 %back.1 = f32[15,8,2,1280]{3,2,1,0:T(2,128)} custom-call(f32[512,128]{1,0:T(8,128)S(1)} %bitcast.5, bf16[512,1280]{1,0:T(8,128)(2,1)S(1)} %get-tuple-element.11.high_ref, bf16[512,1280]{1,0:T(8,128)(2,1)S(1)} %get-tuple-element.12.low_ref), custom_call_target="tpu_custom_call" | custom-call | flops 500000000 | bytes 4000000 | tf_op jit(solution)/shard_map/back/pallas_call | solution.py:492
Async XLA Ops:
  0.0 17.7 %copy-start = (s32[32]{0:T(128)S(1)}, s32[32]{0:T(128)}, u32[]{:S(2)}) copy-start(s32[32]{0:T(128)} %row_ref.1) | copy-start | bytes 388
  6.2 22.3 %all-to-all-start = ((f32[128,4,128]{2,1,0:T(4,128)}), f32[128,4,128]{2,1,0:T(4,128)S(1)}, u32[]{:S(2)}, u32[]{:S(2)}) async-start(f32[128,4,128]{2,1,0:T(4,128)} %bitcast.6), calls=%async_computation | async-start | bytes 524288 | tf_op jit(solution)/shard_map/all_to_all | solution.py:476
  17.7 0.7 %copy-start.1 = (f32[16,128]{1,0:T(8,128)S(1)}, f32[16,128]{1,0:T(8,128)}, u32[]{:S(2)}) copy-start(f32[16,128]{1,0:T(8,128)} %get-tuple-element.10.wave_ref) | copy-start | bytes 24580

commit v3 on v2

--- a/solution.py
+++ b/solution.py
@@ -101,9 +101,9 @@
 
 def front_kernel(
     fields_hbm, sun_hbm, ground_hbm, gas_hbm, weight_hbm, lit_hbm, row_hbm, owner_hbm,
-    out_hbm, wave_ref,
+    out_hbm, wave_hbm,
     fields_ref, sun_ref, ground_ref, gas_ref, weight_ref, lit_ref, row_ref, owner_ref,
-    out_s, pick_s, gas_s, weight_s, left_s, spec_s, turn_s, in_sems, out_sems,
+    out_s, pick_s, share_s, beam_s, left_s, spec_s, turn_s, wave_ref, in_sems, out_sems,
 ):
     lat_me = lax.axis_index("lat")
     lon_me = lax.axis_index("lon")
@@ -124,77 +124,127 @@
         copy.start()
     slot_picks(pick_s)
     arrivals[0].wait()
-    find_slots(owner_ref, pick_s, wave_ref)
     for copy in arrivals[1:]:
         copy.wait()
+    find_slots(owner_ref, pick_s, wave_ref)
+    departures = [pltpu.make_async_copy(wave_ref, wave_hbm, out_sems.at[4])]
+    departures[0].start()
 
     def column(row):
-        padded = jnp.concatenate([row, jnp.zeros((1, 128 - G), f32)], axis=1)
+        padded = jnp.concatenate([row, jnp.ones((1, 128 - G), f32)], axis=1)
         return jnp.broadcast_to(padded, (128, 128)).T
 
+    def thirds(x):
+        first = x.astype(bf16).astype(f32)
+        second = (x - first).astype(bf16).astype(f32)
+        return first, second, (x - first - second).astype(bf16).astype(f32)
+
+    kinds = 2 * LEV
     total_weight = jnp.sum(weight_ref[...], axis=1, keepdims=True)
-    gas_s[...] = column(gas_ref[...])
-    weight_s[...] = column(weight_ref[...] * (heat_gain / total_weight))
+    gas = column(gas_ref[...])
+    share = column(weight_ref[...] * (heat_gain / total_weight))
+    beam_s[...] = share
+    gas_1, gas_2, gas_3 = thirds(gas)
+    log_1, log_2, log_3 = thirds(jnp.log2(share))
+    lane = iota((8, 128), 1)
+    term = lane // kinds
+    for part in range(G // 8):
+        rows = slice(part * 8, (part + 1) * 8)
+        factor = jnp.where(
+            (term == 1) | (term == 4), gas_2[rows], jnp.where(term == 2, gas_3[rows], gas_1[rows])
+        )
+        tail = jnp.where(
+            lane < 6 * kinds + 3,
+            1.0,
+            jnp.where(
+                lane == 6 * kinds + 3,
+                log_1[rows],
+                jnp.where(lane == 6 * kinds + 4, log_2[rows], log_3[rows]),
+            ),
+        )
+        tail = jnp.where((term == 6) & (lane < 6 * kinds + 6), tail, 0.0)
+        pieces = []
+        for kind in range(kinds):
+            own = jnp.where((lane % kinds == kind) & (term < 6), factor, 0.0)
+            pieces.append(jnp.where(term == 6, tail, own) if kind < LEV else own)
+        share_s[part * 64 : (part + 1) * 64, :] = jnp.concatenate(pieces, axis=0).astype(bf16)
 
     counts = []
     for g in range(ROWS_DEV):
         row = row_ref[lat_me * ROWS_DEV + g]
         counts.append(20 + 4 * jnp.minimum(row, NLAT_FULL - 1 - row))
 
-    for g in range(ROWS_DEV):
-
-        def heat_block(a, carry, g=g):
-            columns = pl.ds(pl.multiple_of(a * BLOCK, BLOCK), BLOCK)
+    sub = iota((8, BLOCK), 0)
+    tile = lambda row: jnp.broadcast_to(row, (8, BLOCK))
+    for a in range(SEG_BLOCKS):
+        columns = slice(a * BLOCK, (a + 1) * BLOCK)
+        paths, grounds, suns = [], [], []
+        for g in range(ROWS_DEV):
             x = fields_ref[g, :, columns]
             depth = jnp.maximum(x, 0.0) + jnp.log1p(jnp.exp(-jnp.abs(x)))
             sun = sun_ref[g : g + 1, columns]
-            slant = depth * (-LOG2E / sun)
-            diffuse = depth * (-LOG2E * diffusivity)
-            tile = lambda row: jnp.broadcast_to(row, (8, BLOCK))
-            sun_b = tile(sun * scatter_share)
-            ground = ground_ref[g : g + 1, columns]
-            ground_b = tile(ground)
-            slants = [tile(slant[level : level + 1]) for level in range(LEV)]
-            diffuses = [tile(diffuse[level : level + 1]) for level in range(LEV)]
-            nets = [jnp.zeros((8, BLOCK), f32) for _ in range(LEV + 1)]
-            beams = [jnp.zeros((8, BLOCK), f32) for _ in range(LEV + 1)]
-            for part in range(G // 8):
-                gas = gas_s[part * 8 : (part + 1) * 8, :]
-                beam = sun_b * weight_s[part * 8 : (part + 1) * 8, :]
-                beams[0] = beams[0] + beam
-                down, downs, sources, passed = None, [], [], []
+            suns.append(sun)
+            grounds.append(ground_ref[g : g + 1, columns])
+            slant = tile(depth[:1])
+            for level in range(1, LEV):
+                slant = slant + jnp.where(sub >= level, tile(depth[level : level + 1]), 0.0)
+            path = jnp.where(
+                sub < LEV,
+                slant * (-LOG2E / sun),
+                pltpu.roll(depth, LEV, 0) * (-LOG2E * diffusivity),
+            )
+            path_1, path_2, path_3 = thirds(path)
+            logs = thirds(tile(jnp.log2(sun * scatter_share)))
+            tail = jnp.where(
+                sub == 0, logs[0], jnp.where(sub == 1, logs[1], jnp.where(sub == 2, logs[2], 1.0))
+            )
+            zero = jnp.zeros((8, BLOCK), f32)
+            stack = [path_1, path_1, path_1, path_2, path_2, path_3, tail] + [zero] * 9
+            paths.append(jnp.concatenate(stack, axis=0).astype(bf16))
+        right = jnp.concatenate(paths, axis=1)
+        nets = [[jnp.zeros((8, BLOCK), f32) for _ in range(LEV + 1)] for _ in range(ROWS_DEV)]
+        beams = [[jnp.zeros((8, BLOCK), f32) for _ in range(LEV + 1)] for _ in range(ROWS_DEV)]
+        for g in range(ROWS_DEV):
+            beams[g][0] = tile(suns[g] * (scatter_share * heat_gain / 8))
+        ground_b = [tile(ground) for ground in grounds]
+        sun_b = [tile(sun * scatter_share) for sun in suns]
+        for part in range(G // 8):
+            passing = jnp.exp2(dot(share_s[part * 64 : (part + 1) * 64, :], right))
+            for g in range(ROWS_DEV):
+                net, beam_sum = nets[g], beams[g]
+                pick = lambda kind: passing[kind * 8 : kind * 8 + 8, g * BLOCK : (g + 1) * BLOCK]
+                beam = sun_b[g] * beam_s[part * 8 : (part + 1) * 8, :]
+                down, downs, sources = None, [], []
                 for level in range(LEV):
-                    after = beam * jnp.exp2(gas * slants[level])
+                    after = pick(level)
                     source = beam - after
                     beam = after
-                    t_dif = jnp.exp2(gas * diffuses[level])
-                    down = source if down is None else down * t_dif + source
-                    beams[level + 1] = beams[level + 1] + beam
+                    down = source if down is None else down * pick(LEV + level) + source
+                    beam_sum[level + 1] = beam_sum[level + 1] + beam
                     downs.append(down)
                     sources.append(source)
-                    passed.append(t_dif)
-                nets[LEV] = nets[LEV] + down
-                upward = ground_b * (beam * (1.0 / scatter_share) + down)
+                net[LEV] = net[LEV] + down
+                upward = ground_b[g] * (beam * (1.0 / scatter_share) + down)
                 for level in range(LEV - 1, -1, -1):
-                    upward = upward * passed[level] + sources[level]
+                    upward = upward * pick(LEV + level) + sources[level]
                     if level:
-                        nets[level] = nets[level] + (downs[level - 1] - upward)
+                        net[level] = net[level] + (downs[level - 1] - upward)
                     else:
-                        nets[level] = nets[level] - upward
-            nets = [net + beams[level] * (1.0 / scatter_share) for level, net in enumerate(nets)]
-            nets[LEV] = nets[LEV] * (1.0 - ground)
-            sums = [nets[level] - nets[level + 1] for level in range(LEV)]
+                        net[level] = net[level] - upward
+        for g in range(ROWS_DEV):
+            levels = [
+                net + beam_sum * (1.0 / scatter_share) for net, beam_sum in zip(nets[g], beams[g])
+            ]
+            levels[LEV] = levels[LEV] * (1.0 - grounds[g])
             is_lit = lit_ref[g, a] >= 0
-            heated = x
+            heated = fields_ref[g, :, columns]
             for level in range(LEV):
-                heat = jnp.where(is_lit, jnp.sum(sums[level], axis=0, keepdims=True), 0.0)
-                heated = heated + jnp.where(iota((8, BLOCK), 0) == LEV + level, heat, 0.0)
+                heat = jnp.sum(levels[level] - levels[level + 1], axis=0, keepdims=True)
+                heat = jnp.where(is_lit, heat, 0.0)
+                heated = heated + jnp.where(sub == LEV + level, heat, 0.0)
             first = (lon_me * SEG_BLOCKS + a) * BLOCK
             heated = jnp.where(iota((8, BLOCK), 1) + first < counts[g], heated, 0.0)
-            left_s[g, pl.ds(pl.multiple_of(a * 8, 8), 8), :] = heated
-            return carry
-
-        lax.fori_loop(0, SEG_BLOCKS, heat_block, 0)
+            left_s[g, a * 8 : (a + 1) * 8, :] = heated
 
     offset, place = iota((BLOCK, BLOCK), 0), iota((BLOCK, BLOCK), 1)
     half = BLOCK // 2
@@ -237,7 +287,6 @@
         axis=0,
     )
     steps = jnp.where(iota((24, 128), 0) < 16 + SEG_BLOCKS, steps, 0.0)
-    departures = []
     for lat_group in range(4):
         lanes = slice(lat_group * 128, (lat_group + 1) * 128)
         for pair in range(2):
@@ -440,7 +489,7 @@
             jax.ShapeDtypeStruct((16, 128), f32),
         ),
         in_specs=[hbm] * 8,
-        out_specs=(hbm, vmem),
+        out_specs=(hbm, hbm),
         scratch_shapes=[
             pltpu.VMEM((ROWS_DEV, K, SEG_BLOCKS * BLOCK), f32),
             pltpu.VMEM((ROWS_DEV, SEG_BLOCKS * BLOCK), f32),
@@ -452,13 +501,14 @@
             pltpu.VMEM((MW // 128, 128), jnp.int32),
             pltpu.VMEM((DESTS * 4, 128), f32),
             pltpu.VMEM((4, 128, 128), bf16),
-            pltpu.VMEM((128, 128), f32),
+            pltpu.VMEM((G * 8, 128), bf16),
             pltpu.VMEM((128, 128), f32),
             pltpu.VMEM((ROWS_DEV, SEG_BLOCKS * 8, 128), f32),
             pltpu.VMEM((128, 512), f32),
             pltpu.VMEM((1024, 128), f32),
+            pltpu.VMEM((16, 128), f32),
             pltpu.SemaphoreType.DMA((9,)),
-            pltpu.SemaphoreType.DMA((4,)),
+            pltpu.SemaphoreType.DMA((5,)),
         ],
         cost_estimate=pl.CostEstimate(flops=2 * 10**8, bytes_accessed=10**6, transcendentals=10**6),
         name="front",

time: 30.4 us -> 29.2 us (0.961)
  Pallas kernels: 13.1 us -> 11.9 us
    pallas_call x1, Pallas kernels: 6.22 us -> 4.93 us  [shards(): pl.pallas_call(front_kernel, out_shape=(jax.ShapeDtypeStruct((DESTS * 4,...]
  transfers between devices with their start and end apart: 1 -> 1, of which waited for: 1 -> 1; matrix products, arithmetic and copies ran while one was open for 0% -> 0% of each run, Pallas kernels for 17% -> 18%
where the time goes in v3:
time: 29.2 us; the launch traced here: 28.9 us
  Pallas kernels  11.9 us (41%)
  starting transfers between devices  11.5 us (39%)
  waiting for transfers between devices  4.82 us (17%)
  local copies, waits for them, and re-layouts  0.69 us (2%)
    all_to_all x1, starting transfers between devices, shards(): lax.all_to_all(outgoing.reshape(DESTS, 4, 128), ('lat', 'lon'), split_axi...  11.5 us
    pallas_call x1, Pallas kernels, shards(): pl.pallas_call(recur_kernel, out_shape=(jax.ShapeDtypeStruct((512, MW), b...  5.27 us
    pallas_call x1, Pallas kernels, shards(): pl.pallas_call(front_kernel, out_shape=(jax.ShapeDtypeStruct((DESTS * 4,...  4.93 us
    all_to_all x1, waiting for transfers between devices, shards(): lax.all_to_all(outgoing.reshape(DESTS, 4, 128), ('lat', 'lon'), split_axi...  4.82 us
    pallas_call x1, Pallas kernels, shards(): pl.pallas_call(back_kernel, out_shape=jax.ShapeDtypeStruct((PER_DEV, K, 2...  1.66 us
    unnamed x4, local copies, waits for them, and re-layouts  0.69 us
  transfers between devices with their start and end apart: 1, of which 1 were waited for; matrix products, arithmetic and copies ran while one was open for 0% of the time, Pallas kernels for 18%

profile of v3, /device:TPU:1, one launch (start us, length us, event | category | flops | bytes accessed | tf_op | source)
XLA Modules:
  0.0 28.9 jit_solution(15563930310071937835)
XLA Ops:
  0.0 0.0 copy-start
  0.0 4.9 %front.1 = (f32[512,128]{1,0:T(8,128)}, f32[16,128]{1,0:T(8,128)}) custom-call(f32[8,2,768]{2,1,0:T(2,128)} %fields_hbm.1, f32[2,768]{1,0:T(2,128)} %sun_hbm.1, f32[2,768]{1,0:T(2,128)} %ground_hbm.1, f32[1,112]{1,0:T(1,128)} %bitcast.8, f32[1,112]{1,0:T(1,128)} %bitcast.9, s32[2,6]{1,0:T(2,128)} %lit_hbm.1, s32[32]{0:T(128)} %row_ref.1, s32[10,128]{1,0:T(8,128)} %bitcast.7), custom_call_target="tpu_custom_call" | custom-call | flops 200000000 | bytes 1000000 | tf_op jit(solution)/shard_map/front/pallas_call | solution.py:485
  4.9 11.5 %all-to-all-start = ((f32[128,4,128]{2,1,0:T(4,128)}), f32[128,4,128]{2,1,0:T(4,128)S(1)}, u32[]{:S(2)}, u32[]{:S(2)}) async-start(f32[128,4,128]{2,1,0:T(4,128)} %bitcast.6), calls=%async_computation | async-start | bytes 524288 | tf_op jit(solution)/shard_map/all_to_all | solution.py:526
  16.4 0.0 copy-done
  16.5 0.0 copy-start.1
  16.5 0.7 %copy-done.1 = f32[16,128]{1,0:T(8,128)S(1)} copy-done((f32[16,128]{1,0:T(8,128)S(1)}, f32[16,128]{1,0:T(8,128)}, u32[]{:S(2)}) %copy-start.1) | copy-done | bytes 8216
  17.2 5.3 %recur.1 = (bf16[512,1280]{1,0:T(8,128)(2,1)S(1)}, bf16[512,1280]{1,0:T(8,128)(2,1)S(1)}) custom-call(f32[16,128]{1,0:T(8,128)S(1)} %copy-done.1, s32[32]{0:T(128)S(1)} %copy-done), custom_call_target="tpu_custom_call" | custom-call | flops 20000000 | bytes 3000000 | tf_op jit(solution)/shard_map/recur/pallas_call | solution.py:529
  22.4 4.8 %all-to-all-done = f32[128,4,128]{2,1,0:T(4,128)S(1)} async-done(((f32[128,4,128]{2,1,0:T(4,128)}), f32[128,4,128]{2,1,0:T(4,128)S(1)}, u32[]{:S(2)}, u32[]{:S(2)}) %all-to-all-start) | async-done | bytes 262176 | tf_op jit(solution)/shard_map/all_to_all | solution.py:526
  27.2 1.7 %back.1 = f32[15,8,2,1280]{3,2,1,0:T(2,128)} custom-call(f32[512,128]{1,0:T(8,128)S(1)} %bitcast.5, bf16[512,1280]{1,0:T(8,128)(2,1)S(1)} %get-tuple-element.11.high_ref, bf16[512,1280]{1,0:T(8,128)(2,1)S(1)} %get-tuple-element.12.low_ref), custom_call_target="tpu_custom_call" | custom-call | flops 500000000 | bytes 4000000 | tf_op jit(solution)/shard_map/back/pallas_call | solution.py:542
Async XLA Ops:
  0.0 16.4 %copy-start = (s32[32]{0:T(128)S(1)}, s32[32]{0:T(128)}, u32[]{:S(2)}) copy-start(s32[32]{0:T(128)} %row_ref.1) | copy-start | bytes 388
  4.9 22.3 %all-to-all-start = ((f32[128,4,128]{2,1,0:T(4,128)}), f32[128,4,128]{2,1,0:T(4,128)S(1)}, u32[]{:S(2)}, u32[]{:S(2)}) async-start(f32[128,4,128]{2,1,0:T(4,128)} %bitcast.6), calls=%async_computation | async-start | bytes 524288 | tf_op jit(solution)/shard_map/all_to_all | solution.py:526
  16.5 0.7 %copy-start.1 = (f32[16,128]{1,0:T(8,128)S(1)}, f32[16,128]{1,0:T(8,128)}, u32[]{:S(2)}) copy-start(f32[16,128]{1,0:T(8,128)} %get-tuple-element.10.wave_ref) | copy-start | bytes 24580

commit v4 on v3

--- a/solution.py
+++ b/solution.py
@@ -62,16 +62,17 @@
     lane = iota((128, 128), 1)
     for u in range(4):
         index = slot_of(lane % 4, u)
-        rank = ((lane // 4) % N_LON) * PER_DEV + index
-        pick = (iota((128, 128), 0) == rank) & (index < PER_DEV)
-        pick_ref[u] = pick.astype(f32).astype(bf16)
-
-
-def find_slots(owner_ref, pick_ref, wave_ref):
+        for kind, span in enumerate((N_LON, N_LON // 2)):
+            rank = ((lane // 4) % span) * PER_DEV + index
+            pick = (iota((128, 128), 0) == rank) & (index < PER_DEV)
+            pick_ref[kind * 4 + u] = pick.astype(f32).astype(bf16)
+
+
+def find_slots(owner_ref, pick_ref, table_ref, order_ref, wave_ref):
     groups = MW // 128
-    hits = [
-        (owner_ref[b : b + 1, :] == iota((N_LAT, 128), 0)).astype(f32) for b in range(groups)
-    ]
+    owner = iota((N_LAT, 128), 0)
+    lane = iota((N_LAT, 128), 1)
+    hits = [(owner_ref[b : b + 1, :] == owner).astype(f32) for b in range(groups)]
     stacked = jnp.concatenate(hits, axis=0).astype(bf16)
     before = (iota((128, 128), 0) < iota((128, 128), 1)).astype(f32).astype(bf16)
     ahead = dot(stacked, before)
@@ -83,27 +84,35 @@
         rank = jnp.sum(hits[b] * (ahead[part] + carry), axis=0, keepdims=True)
         carry = carry + total[part]
         ranked = (rank.astype(jnp.int32) == iota((128, 128), 0)).astype(f32).astype(bf16)
-        number = iota((N_LAT, 128), 1) + (b * 128 + 1)
+        number = lane + (b * 128 + 1)
         high = ((number >> 4) << 4).astype(f32)
         low = (number & 15).astype(f32)
         both = jnp.concatenate([hits[b] * high, hits[b] * low], axis=0).astype(bf16)
         table = table + dot(both, ranked, (1, 1))
+    table_ref[...] = table
+    full = carry > (MCAP * 2 / 3)
+    below = (iota((N_LAT, N_LAT), 1) < iota((N_LAT, N_LAT), 0)).astype(f32).astype(bf16)
+    fulls = dot(below, full.astype(f32).astype(bf16))
+    spare = owner.astype(f32) - fulls + N_LAT // 2
+    place = jnp.where(full, fulls, spare).astype(jnp.int32)
+    order_ref[...] = jnp.sum(jnp.where(place == lane, owner, 0), axis=0, keepdims=True)
     table = table.astype(bf16)
     for u in range(4):
-        found = dot(table, pick_ref[u])
-        found = found[:N_LAT] + found[N_LAT:]
-        for g in range(4):
-            own = iota((N_LAT, 128), 0) == g * 4 + iota((N_LAT, 128), 1) // 32
-            wave_ref[u * 4 + g : u * 4 + g + 1, :] = jnp.sum(
-                jnp.where(own, found, 0.0), axis=0, keepdims=True
-            )
+        for kind in range(2):
+            found = dot(table, pick_ref[kind * 4 + u])
+            found = found[:N_LAT] + found[N_LAT:]
+            for g in (0, 1) if kind == 0 else (2,):
+                own = place == (g * 4 + lane // 32 if kind == 0 else 8 + lane // 16)
+                wave_ref[u * 4 + g : u * 4 + g + 1, :] = jnp.sum(
+                    jnp.where(own, found, 0.0), axis=0, keepdims=True
+                )
 
 
 def front_kernel(
     fields_hbm, sun_hbm, ground_hbm, gas_hbm, weight_hbm, lit_hbm, row_hbm, owner_hbm,
-    out_hbm, wave_hbm,
+    out_hbm, table_hbm,
     fields_ref, sun_ref, ground_ref, gas_ref, weight_ref, lit_ref, row_ref, owner_ref,
-    out_s, pick_s, share_s, beam_s, left_s, spec_s, turn_s, wave_ref, in_sems, out_sems,
+    out_s, pick_s, share_s, beam_s, left_s, spec_s, turn_s, wave_ref, table_s, row_s, order_s, turned_s, in_sems, out_sems,
 ):
     lat_me = lax.axis_index("lat")
     lon_me = lax.axis_index("lon")
@@ -123,12 +132,11 @@
     for copy in arrivals:
         copy.start()
     slot_picks(pick_s)
+    out_s[...] = jnp.zeros_like(out_s)
     arrivals[0].wait()
     for copy in arrivals[1:]:
         copy.wait()
-    find_slots(owner_ref, pick_s, wave_ref)
-    departures = [pltpu.make_async_copy(wave_ref, wave_hbm, out_sems.at[4])]
-    departures[0].start()
+    find_slots(owner_ref, pick_s, table_s, row_s, wave_ref)
 
     def column(row):
         padded = jnp.concatenate([row, jnp.ones((1, 128 - G), f32)], axis=1)
@@ -287,7 +295,7 @@
         axis=0,
     )
     steps = jnp.where(iota((24, 128), 0) < 16 + SEG_BLOCKS, steps, 0.0)
-    for lat_group in range(4):
+    for lat_group in range(3):
         lanes = slice(lat_group * 128, (lat_group + 1) * 128)
         for pair in range(2):
             for g in range(ROWS_DEV):
@@ -338,19 +346,27 @@
                         imag = imag - (cos_a * s + sin_a * c)
                     row = u * 32 + g * 16
                     spec_s[row : row + 16, lanes] = jnp.concatenate([real, imag], axis=0)
-        out_s[lanes, :] = spec_s[:, lanes].T
-        copy = pltpu.make_async_copy(out_s.at[lanes, :], out_hbm.at[lanes, :], out_sems.at[lat_group])
-        copy.start()
-        departures.append(copy)
-    for copy in departures:
-        copy.wait()
-
-
-def recur_kernel(wave_ref, row_ref, high_ref, low_ref, poly_s):
+        turned_s[lanes, :] = spec_s[:, lanes].T
+        if lat_group == 0:
+            ordering = pltpu.make_async_copy(row_s, order_s, in_sems.at[9])
+            leaving = pltpu.make_async_copy(table_s, table_hbm, out_sems.at[0])
+            ordering.start()
+            leaving.start()
+    ordering.wait()
+    for place in range(N_LAT):
+        span = 32 if place < 8 else 16
+        first = place * 32 if place < 8 else 256 + (place - 8) * 16
+        start = pl.multiple_of(order_s[0, place] * 32, 32)
+        out_s[pl.ds(start, span), :] = turned_s[first : first + span, :]
+    sending = pltpu.make_async_copy(out_s, out_hbm, out_sems.at[1])
+    sending.start()
+    leaving.wait()
+    sending.wait()
+
+
+def recur_kernel(table_ref, row_ref, high_ref, low_ref, poly_s):
     lat_me = lax.axis_index("lat")
     lon_me = lax.axis_index("lon")
-    me = lat_me * N_LON + lon_me
-    group = me // 32
     lane = iota((1, 128), 1)
     rows = jnp.zeros((1, 128), jnp.int32)
     for part in range(ROWS_DEV):
@@ -360,16 +376,14 @@
     _, x = sincos_quarter(jnp.broadcast_to(angle * (math.pi / (4 * NLAT_FULL)), (4, 128)))
     log_sin = 0.5 * jnp.log1p(-x * x)
 
+    table = table_ref[...].astype(bf16)
     found = []
     for q in range(4):
-        total = jnp.zeros((1, 128), f32)
-        for u in range(4):
-            mine = wave_ref[pl.ds(u * 4 + group, 1), :]
-            value = jnp.sum(
-                jnp.where(lane == (me % 32) * 4 + q, mine, 0.0), axis=1, keepdims=True
-            )
-            total = jnp.where(lane // 32 == u, value, total)
-        found.append(total)
+        index = slot_of(q, iota((128, 128), 1) // 32)
+        pick = (iota((128, 128), 0) == lon_me * PER_DEV + index) & (index < PER_DEV)
+        both = dot(table, pick.astype(f32).astype(bf16))
+        mine = jnp.where(iota((N_LAT, 128), 0) == lat_me, both[:N_LAT] + both[N_LAT:], 0.0)
+        found.append(jnp.sum(mine, axis=0, keepdims=True))
     number = jnp.concatenate(found, axis=0)
     m = jnp.maximum(number - 1.0, 0.0)
     limit = jnp.where(number > 0.5, MW - m, 0.0)
@@ -482,11 +496,11 @@
     smem = pl.BlockSpec(memory_space=pltpu.SMEM)
     hbm = pl.BlockSpec(memory_space=pl.ANY)
     limits = pltpu.CompilerParams(vmem_limit_bytes=16 * 2**20)
-    outgoing, waves = pl.pallas_call(
+    outgoing, table = pl.pallas_call(
         front_kernel,
         out_shape=(
             jax.ShapeDtypeStruct((DESTS * 4, 128), f32),
-            jax.ShapeDtypeStruct((16, 128), f32),
+            jax.ShapeDtypeStruct((2 * N_LAT, 128), f32),
         ),
         in_specs=[hbm] * 8,
         out_specs=(hbm, hbm),
@@ -500,15 +514,19 @@
             pltpu.SMEM((ROWS_T,), jnp.int32),
             pltpu.VMEM((MW // 128, 128), jnp.int32),
             pltpu.VMEM((DESTS * 4, 128), f32),
-            pltpu.VMEM((4, 128, 128), bf16),
+            pltpu.VMEM((8, 128, 128), bf16),
             pltpu.VMEM((G * 8, 128), bf16),
             pltpu.VMEM((128, 128), f32),
             pltpu.VMEM((ROWS_DEV, SEG_BLOCKS * 8, 128), f32),
-            pltpu.VMEM((128, 512), f32),
+            pltpu.VMEM((128, 384), f32),
             pltpu.VMEM((1024, 128), f32),
             pltpu.VMEM((16, 128), f32),
-            pltpu.SemaphoreType.DMA((9,)),
-            pltpu.SemaphoreType.DMA((5,)),
+            pltpu.VMEM((2 * N_LAT, 128), f32),
+            pltpu.VMEM((1, 128), jnp.int32),
+            pltpu.SMEM((1, 128), jnp.int32),
+            pltpu.VMEM((DESTS * 3, 128), f32),
+            pltpu.SemaphoreType.DMA((10,)),
+            pltpu.SemaphoreType.DMA((2,)),
         ],
         cost_estimate=pl.CostEstimate(flops=2 * 10**8, bytes_accessed=10**6, transcendentals=10**6),
         name="front",
@@ -538,7 +556,7 @@
         cost_estimate=pl.CostEstimate(flops=2 * 10**7, bytes_accessed=3 * 10**6, transcendentals=10**6),
         name="recur",
         compiler_params=limits,
-    )(waves, row_lat)
+    )(table, row_lat)
     return pl.pallas_call(
         back_kernel,
         out_shape=jax.ShapeDtypeStruct((PER_DEV, K, 2, MW), f32),

time: 29.2 us -> 28.9 us (0.990)
  transfers between devices with their start and end apart: 1 -> 1, of which waited for: 1 -> 1; matrix products, arithmetic and copies ran while one was open for 0% -> 0% of each run, Pallas kernels for 18% -> 19%
where the time goes in v4:
time: 28.9 us; the launch traced here: 28.7 us
  Pallas kernels  11.7 us (40%)
  starting transfers between devices  11.5 us (40%)
  waiting for transfers between devices  4.74 us (16%)
  local copies, waits for them, and re-layouts  0.71 us (2%)
    all_to_all x1, starting transfers between devices, shards(): lax.all_to_all(outgoing.reshape(DESTS, 4, 128), ('lat', 'lon'), split_axi...  11.5 us
    pallas_call x1, Pallas kernels, shards(): pl.pallas_call(recur_kernel, out_shape=(jax.ShapeDtypeStruct((512, MW), b...  5.33 us
    all_to_all x1, waiting for transfers between devices, shards(): lax.all_to_all(outgoing.reshape(DESTS, 4, 128), ('lat', 'lon'), split_axi...  4.74 us
    pallas_call x1, Pallas kernels, shards(): pl.pallas_call(front_kernel, out_shape=(jax.ShapeDtypeStruct((DESTS * 4,...  4.69 us
    pallas_call x1, Pallas kernels, shards(): pl.pallas_call(back_kernel, out_shape=jax.ShapeDtypeStruct((PER_DEV, K, 2...  1.66 us
    unnamed x4, local copies, waits for them, and re-layouts  0.71 us
  transfers between devices with their start and end apart: 1, of which 1 were waited for; matrix products, arithmetic and copies ran while one was open for 0% of the time, Pallas kernels for 19%

profile of v4, /device:TPU:1, one launch (start us, length us, event | category | flops | bytes accessed | tf_op | source)
XLA Modules:
  0.0 28.7 jit_solution(15736326848751180043)
XLA Ops:
  0.0 0.0 copy-start
  0.0 4.7 %front.1 = (f32[512,128]{1,0:T(8,128)}, f32[32,128]{1,0:T(8,128)}) custom-call(f32[8,2,768]{2,1,0:T(2,128)} %fields_hbm.1, f32[2,768]{1,0:T(2,128)} %sun_hbm.1, f32[2,768]{1,0:T(2,128)} %ground_hbm.1, f32[1,112]{1,0:T(1,128)} %bitcast.8, f32[1,112]{1,0:T(1,128)} %bitcast.9, s32[2,6]{1,0:T(2,128)} %lit_hbm.1, s32[32]{0:T(128)} %row_ref.1, s32[10,128]{1,0:T(8,128)} %bitcast.7), custom_call_target="tpu_custom_call" | custom-call | flops 200000000 | bytes 1000000 | tf_op jit(solution)/shard_map/front/pallas_call | solution.py:499
  4.7 11.5 %all-to-all-start = ((f32[128,4,128]{2,1,0:T(4,128)}), f32[128,4,128]{2,1,0:T(4,128)S(1)}, u32[]{:S(2)}, u32[]{:S(2)}) async-start(f32[128,4,128]{2,1,0:T(4,128)} %bitcast.6), calls=%async_computation | async-start | bytes 524288 | tf_op jit(solution)/shard_map/all_to_all | solution.py:544
  16.2 0.0 copy-done
  16.2 0.0 copy-start.1
  16.2 0.7 %copy-done.1 = f32[32,128]{1,0:T(8,128)S(1)} copy-done((f32[32,128]{1,0:T(8,128)S(1)}, f32[32,128]{1,0:T(8,128)}, u32[]{:S(2)}) %copy-start.1) | copy-done | bytes 16408
  16.9 5.3 %recur.1 = (bf16[512,1280]{1,0:T(8,128)(2,1)S(1)}, bf16[512,1280]{1,0:T(8,128)(2,1)S(1)}) custom-call(f32[32,128]{1,0:T(8,128)S(1)} %copy-done.1, s32[32]{0:T(128)S(1)} %copy-done), custom_call_target="tpu_custom_call" | custom-call | flops 20000000 | bytes 3000000 | tf_op jit(solution)/shard_map/recur/pallas_call | solution.py:547
  22.3 4.7 %all-to-all-done = f32[128,4,128]{2,1,0:T(4,128)S(1)} async-done(((f32[128,4,128]{2,1,0:T(4,128)}), f32[128,4,128]{2,1,0:T(4,128)S(1)}, u32[]{:S(2)}, u32[]{:S(2)}) %all-to-all-start) | async-done | bytes 262176 | tf_op jit(solution)/shard_map/all_to_all | solution.py:544
  27.0 1.7 %back.1 = f32[15,8,2,1280]{3,2,1,0:T(2,128)} custom-call(f32[512,128]{1,0:T(8,128)S(1)} %bitcast.5, bf16[512,1280]{1,0:T(8,128)(2,1)S(1)} %get-tuple-element.11.high_ref, bf16[512,1280]{1,0:T(8,128)(2,1)S(1)} %get-tuple-element.12.low_ref), custom_call_target="tpu_custom_call" | custom-call | flops 500000000 | bytes 4000000 | tf_op jit(solution)/shard_map/back/pallas_call | solution.py:560
Async XLA Ops:
  0.0 16.2 %copy-start = (s32[32]{0:T(128)S(1)}, s32[32]{0:T(128)}, u32[]{:S(2)}) copy-start(s32[32]{0:T(128)} %row_ref.1) | copy-start | bytes 388
  4.7 22.3 %all-to-all-start = ((f32[128,4,128]{2,1,0:T(4,128)}), f32[128,4,128]{2,1,0:T(4,128)S(1)}, u32[]{:S(2)}, u32[]{:S(2)}) async-start(f32[128,4,128]{2,1,0:T(4,128)} %bitcast.6), calls=%async_computation | async-start | bytes 524288 | tf_op jit(solution)/shard_map/all_to_all | solution.py:544
  16.2 0.7 %copy-start.1 = (f32[32,128]{1,0:T(8,128)S(1)}, f32[32,128]{1,0:T(8,128)}, u32[]{:S(2)}) copy-start(f32[32,128]{1,0:T(8,128)} %get-tuple-element.10.table_ref) | copy-start | bytes 49156

commit v5 on v4

--- a/solution.py
+++ b/solution.py
@@ -216,11 +216,11 @@
             beams[g][0] = tile(suns[g] * (scatter_share * heat_gain / 8))
         ground_b = [tile(ground) for ground in grounds]
         sun_b = [tile(sun * scatter_share) for sun in suns]
-        for part in range(G // 8):
-            passing = jnp.exp2(dot(share_s[part * 64 : (part + 1) * 64, :], right))
-            for g in range(ROWS_DEV):
+        for g in range(ROWS_DEV):
+            for part in range(G // 8):
+                passing = jnp.exp2(dot(share_s[part * 64 : (part + 1) * 64, :], paths[g]))
                 net, beam_sum = nets[g], beams[g]
-                pick = lambda kind: passing[kind * 8 : kind * 8 + 8, g * BLOCK : (g + 1) * BLOCK]
+                pick = lambda kind: passing[kind * 8 : kind * 8 + 8]
                 beam = sun_b[g] * beam_s[part * 8 : (part + 1) * 8, :]
                 down, downs, sources = None, [], []
                 for level in range(LEV):

time: 28.9 us -> 28.8 us (level)
  no operation moved by 1% of the time
where the time goes in v5:
time: 28.8 us; the launch traced here: 28.6 us
  Pallas kernels  11.6 us (40%)
  starting transfers between devices  11.5 us (40%)
  waiting for transfers between devices  4.74 us (16%)
  local copies, waits for them, and re-layouts  0.71 us (2%)
    all_to_all x1, starting transfers between devices, shards(): lax.all_to_all(outgoing.reshape(DESTS, 4, 128), ('lat', 'lon'), split_axi...  11.5 us
    pallas_call x1, Pallas kernels, shards(): pl.pallas_call(recur_kernel, out_shape=(jax.ShapeDtypeStruct((512, MW), b...  5.33 us
    all_to_all x1, waiting for transfers between devices, shards(): lax.all_to_all(outgoing.reshape(DESTS, 4, 128), ('lat', 'lon'), split_axi...  4.74 us
    pallas_call x1, Pallas kernels, shards(): pl.pallas_call(front_kernel, out_shape=(jax.ShapeDtypeStruct((DESTS * 4,...  4.6 us
    pallas_call x1, Pallas kernels, shards(): pl.pallas_call(back_kernel, out_shape=jax.ShapeDtypeStruct((PER_DEV, K, 2...  1.66 us
    unnamed x4, local copies, waits for them, and re-layouts  0.71 us
  transfers between devices with their start and end apart: 1, of which 1 were waited for; matrix products, arithmetic and copies ran while one was open for 0% of the time, Pallas kernels for 19%

profile of v5, /device:TPU:1, one launch (start us, length us, event | category | flops | bytes accessed | tf_op | source)
XLA Modules:
  0.0 28.6 jit_solution(16658204489735147442)
XLA Ops:
  0.0 0.0 copy-start
  0.0 4.6 %front.1 = (f32[512,128]{1,0:T(8,128)}, f32[32,128]{1,0:T(8,128)}) custom-call(f32[8,2,768]{2,1,0:T(2,128)} %fields_hbm.1, f32[2,768]{1,0:T(2,128)} %sun_hbm.1, f32[2,768]{1,0:T(2,128)} %ground_hbm.1, f32[1,112]{1,0:T(1,128)} %bitcast.8, f32[1,112]{1,0:T(1,128)} %bitcast.9, s32[2,6]{1,0:T(2,128)} %lit_hbm.1, s32[32]{0:T(128)} %row_ref.1, s32[10,128]{1,0:T(8,128)} %bitcast.7), custom_call_target="tpu_custom_call" | custom-call | flops 200000000 | bytes 1000000 | tf_op jit(solution)/shard_map/front/pallas_call | solution.py:499
  4.6 11.5 %all-to-all-start = ((f32[128,4,128]{2,1,0:T(4,128)}), f32[128,4,128]{2,1,0:T(4,128)S(1)}, u32[]{:S(2)}, u32[]{:S(2)}) async-start(f32[128,4,128]{2,1,0:T(4,128)} %bitcast.6), calls=%async_computation | async-start | bytes 524288 | tf_op jit(solution)/shard_map/all_to_all | solution.py:544
  16.1 0.0 copy-done
  16.1 0.0 copy-start.1
  16.1 0.7 %copy-done.1 = f32[32,128]{1,0:T(8,128)S(1)} copy-done((f32[32,128]{1,0:T(8,128)S(1)}, f32[32,128]{1,0:T(8,128)}, u32[]{:S(2)}) %copy-start.1) | copy-done | bytes 16408
  16.8 5.3 %recur.1 = (bf16[512,1280]{1,0:T(8,128)(2,1)S(1)}, bf16[512,1280]{1,0:T(8,128)(2,1)S(1)}) custom-call(f32[32,128]{1,0:T(8,128)S(1)} %copy-done.1, s32[32]{0:T(128)S(1)} %copy-done), custom_call_target="tpu_custom_call" | custom-call | flops 20000000 | bytes 3000000 | tf_op jit(solution)/shard_map/recur/pallas_call | solution.py:547
  22.2 4.7 %all-to-all-done = f32[128,4,128]{2,1,0:T(4,128)S(1)} async-done(((f32[128,4,128]{2,1,0:T(4,128)}), f32[128,4,128]{2,1,0:T(4,128)S(1)}, u32[]{:S(2)}, u32[]{:S(2)}) %all-to-all-start) | async-done | bytes 262176 | tf_op jit(solution)/shard_map/all_to_all | solution.py:544
  26.9 1.7 %back.1 = f32[15,8,2,1280]{3,2,1,0:T(2,128)} custom-call(f32[512,128]{1,0:T(8,128)S(1)} %bitcast.5, bf16[512,1280]{1,0:T(8,128)(2,1)S(1)} %get-tuple-element.11.high_ref, bf16[512,1280]{1,0:T(8,128)(2,1)S(1)} %get-tuple-element.12.low_ref), custom_call_target="tpu_custom_call" | custom-call | flops 500000000 | bytes 4000000 | tf_op jit(solution)/shard_map/back/pallas_call | solution.py:560
Async XLA Ops:
  0.0 16.1 %copy-start = (s32[32]{0:T(128)S(1)}, s32[32]{0:T(128)}, u32[]{:S(2)}) copy-start(s32[32]{0:T(128)} %row_ref.1) | copy-start | bytes 388
  4.6 22.3 %all-to-all-start = ((f32[128,4,128]{2,1,0:T(4,128)}), f32[128,4,128]{2,1,0:T(4,128)S(1)}, u32[]{:S(2)}, u32[]{:S(2)}) async-start(f32[128,4,128]{2,1,0:T(4,128)} %bitcast.6), calls=%async_computation | async-start | bytes 524288 | tf_op jit(solution)/shard_map/all_to_all | solution.py:544
  16.1 0.7 %copy-start.1 = (f32[32,128]{1,0:T(8,128)S(1)}, f32[32,128]{1,0:T(8,128)}, u32[]{:S(2)}) copy-start(f32[32,128]{1,0:T(8,128)} %get-tuple-element.10.table_ref) | copy-start | bytes 49156

commit v6 on v5

--- a/solution.py
+++ b/solution.py
@@ -207,7 +207,7 @@
                 sub == 0, logs[0], jnp.where(sub == 1, logs[1], jnp.where(sub == 2, logs[2], 1.0))
             )
             zero = jnp.zeros((8, BLOCK), f32)
-            stack = [path_1, path_1, path_1, path_2, path_2, path_3, tail] + [zero] * 9
+            stack = [path_1, path_1, path_1, path_2, path_2, path_3, tail] + [zero]
             paths.append(jnp.concatenate(stack, axis=0).astype(bf16))
         right = jnp.concatenate(paths, axis=1)
         nets = [[jnp.zeros((8, BLOCK), f32) for _ in range(LEV + 1)] for _ in range(ROWS_DEV)]
@@ -218,7 +218,7 @@
         sun_b = [tile(sun * scatter_share) for sun in suns]
         for g in range(ROWS_DEV):
             for part in range(G // 8):
-                passing = jnp.exp2(dot(share_s[part * 64 : (part + 1) * 64, :], paths[g]))
+                passing = jnp.exp2(dot(share_s[part * 64 : (part + 1) * 64, :64], paths[g]))
                 net, beam_sum = nets[g], beams[g]
                 pick = lambda kind: passing[kind * 8 : kind * 8 + 8]
                 beam = sun_b[g] * beam_s[part * 8 : (part + 1) * 8, :]
@@ -253,6 +253,11 @@
             first = (lon_me * SEG_BLOCKS + a) * BLOCK
             heated = jnp.where(iota((8, BLOCK), 1) + first < counts[g], heated, 0.0)
             left_s[g, a * 8 : (a + 1) * 8, :] = heated
+
+    ordering = pltpu.make_async_copy(row_s, order_s, in_sems.at[9])
+    leaving = pltpu.make_async_copy(table_s, table_hbm, out_sems.at[0])
+    ordering.start()
+    leaving.start()
 
     offset, place = iota((BLOCK, BLOCK), 0), iota((BLOCK, BLOCK), 1)
     half = BLOCK // 2
@@ -347,11 +352,6 @@
                     row = u * 32 + g * 16
                     spec_s[row : row + 16, lanes] = jnp.concatenate([real, imag], axis=0)
         turned_s[lanes, :] = spec_s[:, lanes].T
-        if lat_group == 0:
-            ordering = pltpu.make_async_copy(row_s, order_s, in_sems.at[9])
-            leaving = pltpu.make_async_copy(table_s, table_hbm, out_sems.at[0])
-            ordering.start()
-            leaving.start()
     ordering.wait()
     for place in range(N_LAT):
         span = 32 if place < 8 else 16

time: 28.8 us -> 28.8 us (level)
  no operation moved by 1% of the time
where the time goes in v6:
time: 28.8 us; the launch traced here: 28.6 us
  Pallas kernels  11.6 us (40%)
  starting transfers between devices  11.5 us (40%)
  waiting for transfers between devices  4.74 us (16%)
  local copies, waits for them, and re-layouts  0.71 us (2%)
    all_to_all x1, starting transfers between devices, shards(): lax.all_to_all(outgoing.reshape(DESTS, 4, 128), ('lat', 'lon'), split_axi...  11.5 us
    pallas_call x1, Pallas kernels, shards(): pl.pallas_call(recur_kernel, out_shape=(jax.ShapeDtypeStruct((512, MW), b...  5.33 us
    all_to_all x1, waiting for transfers between devices, shards(): lax.all_to_all(outgoing.reshape(DESTS, 4, 128), ('lat', 'lon'), split_axi...  4.74 us
    pallas_call x1, Pallas kernels, shards(): pl.pallas_call(front_kernel, out_shape=(jax.ShapeDtypeStruct((DESTS * 4,...  4.6 us
    pallas_call x1, Pallas kernels, shards(): pl.pallas_call(back_kernel, out_shape=jax.ShapeDtypeStruct((PER_DEV, K, 2...  1.65 us
    unnamed x4, local copies, waits for them, and re-layouts  0.71 us
  transfers between devices with their start and end apart: 1, of which 1 were waited for; matrix products, arithmetic and copies ran while one was open for 0% of the time, Pallas kernels for 19%

profile of v6, /device:TPU:1, one launch (start us, length us, event | category | flops | bytes accessed | tf_op | source)
XLA Modules:
  0.0 28.6 jit_solution(1138730406673379197)
XLA Ops:
  0.0 0.0 copy-start
  0.0 4.6 %front.1 = (f32[512,128]{1,0:T(8,128)}, f32[32,128]{1,0:T(8,128)}) custom-call(f32[8,2,768]{2,1,0:T(2,128)} %fields_hbm.1, f32[2,768]{1,0:T(2,128)} %sun_hbm.1, f32[2,768]{1,0:T(2,128)} %ground_hbm.1, f32[1,112]{1,0:T(1,128)} %bitcast.8, f32[1,112]{1,0:T(1,128)} %bitcast.9, s32[2,6]{1,0:T(2,128)} %lit_hbm.1, s32[32]{0:T(128)} %row_ref.1, s32[10,128]{1,0:T(8,128)} %bitcast.7), custom_call_target="tpu_custom_call" | custom-call | flops 200000000 | bytes 1000000 | tf_op jit(solution)/shard_map/front/pallas_call | solution.py:499
  4.6 11.5 %all-to-all-start = ((f32[128,4,128]{2,1,0:T(4,128)}), f32[128,4,128]{2,1,0:T(4,128)S(1)}, u32[]{:S(2)}, u32[]{:S(2)}) async-start(f32[128,4,128]{2,1,0:T(4,128)} %bitcast.6), calls=%async_computation | async-start | bytes 524288 | tf_op jit(solution)/shard_map/all_to_all | solution.py:544
  16.1 0.0 copy-done
  16.1 0.0 copy-start.1
  16.1 0.7 %copy-done.1 = f32[32,128]{1,0:T(8,128)S(1)} copy-done((f32[32,128]{1,0:T(8,128)S(1)}, f32[32,128]{1,0:T(8,128)}, u32[]{:S(2)}) %copy-start.1) | copy-done | bytes 16408
  16.8 5.3 %recur.1 = (bf16[512,1280]{1,0:T(8,128)(2,1)S(1)}, bf16[512,1280]{1,0:T(8,128)(2,1)S(1)}) custom-call(f32[32,128]{1,0:T(8,128)S(1)} %copy-done.1, s32[32]{0:T(128)S(1)} %copy-done), custom_call_target="tpu_custom_call" | custom-call | flops 20000000 | bytes 3000000 | tf_op jit(solution)/shard_map/recur/pallas_call | solution.py:547
  22.2 4.7 %all-to-all-done = f32[128,4,128]{2,1,0:T(4,128)S(1)} async-done(((f32[128,4,128]{2,1,0:T(4,128)}), f32[128,4,128]{2,1,0:T(4,128)S(1)}, u32[]{:S(2)}, u32[]{:S(2)}) %all-to-all-start) | async-done | bytes 262176 | tf_op jit(solution)/shard_map/all_to_all | solution.py:544
  26.9 1.7 %back.1 = f32[15,8,2,1280]{3,2,1,0:T(2,128)} custom-call(f32[512,128]{1,0:T(8,128)S(1)} %bitcast.5, bf16[512,1280]{1,0:T(8,128)(2,1)S(1)} %get-tuple-element.11.high_ref, bf16[512,1280]{1,0:T(8,128)(2,1)S(1)} %get-tuple-element.12.low_ref), custom_call_target="tpu_custom_call" | custom-call | flops 500000000 | bytes 4000000 | tf_op jit(solution)/shard_map/back/pallas_call | solution.py:560
Async XLA Ops:
  0.0 16.1 %copy-start = (s32[32]{0:T(128)S(1)}, s32[32]{0:T(128)}, u32[]{:S(2)}) copy-start(s32[32]{0:T(128)} %row_ref.1) | copy-start | bytes 388
  4.6 22.3 %all-to-all-start = ((f32[128,4,128]{2,1,0:T(4,128)}), f32[128,4,128]{2,1,0:T(4,128)S(1)}, u32[]{:S(2)}, u32[]{:S(2)}) async-start(f32[128,4,128]{2,1,0:T(4,128)} %bitcast.6), calls=%async_computation | async-start | bytes 524288 | tf_op jit(solution)/shard_map/all_to_all | solution.py:544
  16.1 0.7 %copy-start.1 = (f32[32,128]{1,0:T(8,128)S(1)}, f32[32,128]{1,0:T(8,128)}, u32[]{:S(2)}) copy-start(f32[32,128]{1,0:T(8,128)} %get-tuple-element.10.table_ref) | copy-start | bytes 49156
